TPU v7x, 32 devices: a whole 2x2x4 slice. The times are simulated.
32 devices in a mesh: fx: 8 (over z, x), fy: 4 (over y, core).
Axes of the slice: x: 2, y: 2, z: 4, core: 2. Of those that a mesh axis runs over, the one named last changes fastest.
Arguments:
- right_side: float32 [512, 2048], P(('fx', 'fy'))
- coupling: float32 [512, 11, 4096], P(('fx', 'fy')), may hold values from -0.109375 to 0.109375
- face_columns: int32 [512, 11], P(('fx', 'fy')), may hold values from 0 to 31, as said below
- ghost_lists: int32 [128, 4], P(('fx', 'fy')), may hold values from 0 to 15, as said below
Outputs:
- solution: float32 [512, 2048], P(('fx', 'fy'))
- residual: float32 [512, 2048], P(('fx', 'fy'))
Inputs may be any that keep to these rules, and one draw needn't show every extreme that they name: face_columns[f, 0] is f's own index within its block; entries 1 to 6 name other faces of the same block, all distinct and below 16; entries 7 to 10 are distinct and name received faces, 16 + d * 4 + g for the g-th face of group d of the extended list; every received slot of every block is named by some row of that block. `ghost_lists`: each row names 4 distinct faces of its block by local index.
All inputs are finite; a program needn't handle non-finite values.
Results may differ from a plain program's by a relative error of at most 0.0003.
Values sent between devices are 32-bit elements; how exact they have to be, the bound alone decides.
A program may use at most 64 MiB of HBM per device.

v0:
```python
import functools

import jax
import jax.numpy as jnp
from jax import lax
from jax.experimental import pallas as pl
from jax.experimental.pallas import tpu as pltpu
from jax.sharding import PartitionSpec as P

DOF = 64
NRHS = 32
BLOCKS = 11
OWNED = 7
POWERS = 3
LANES = 128
HALF = DOF // 2
UNROLL = 16
GROUPS = LANES // NRHS
MESH = pl.DeviceIdType.MESH
f32 = jnp.float32
bf16 = jnp.bfloat16


def split(x):
    hi = x.astype(bf16).astype(f32)
    return hi, x - hi


def lane_group(rows):
    return lax.broadcasted_iota(jnp.int32, (rows, LANES), 1) // NRHS


def pick(group, parts):
    out = parts[-1]
    for index in range(len(parts) - 2, -1, -1):
        out = jnp.where(group == index, parts[index], out)
    return out


def replicate(group, rolled, source):
    return pick(group, [rolled[(lane - source) % GROUPS] for lane in range(GROUPS)])


def rolls(x):
    return [x] + [pltpu.roll(x, step * NRHS, 1) for step in range(1, GROUPS)]


def product_tile(x, group):
    hi, lo = split(x)
    zero = jnp.zeros_like(x)
    top = pick(group, [hi, zero, lo, zero])
    bottom = pick(group, [zero, hi, zero, lo])
    return top.astype(bf16), bottom.astype(bf16)


def kernel(shape, right_ref, coupling_ref, columns_ref, ghost_ref, sol_ref, res_ref,
           stage, spread, mats, w0, w1, w2, w3, tiles, acc, send_buf, recv_buf,
           zbuf, vbuf, gram_buf, plane_recv, line_recv, final_buf, wide,
           load_sem, send_sem, recv_sem, ps_sem, pr_sem, ls_sem, lr_sem, as_sem, ar_sem):
    n_fx, n_fy, low, faces = shape
    plane = low * n_fy
    high = n_fx // low
    i = lax.axis_index("fx")
    j = lax.axis_index("fy")
    my_low = i % low
    my_high = i // low
    my_rank = my_low * n_fy + j
    fields = [w0, w1, w2, w3]

    def plane_target(offset):
        rank = lax.rem(my_rank + offset, plane)
        return rank, (my_high * low + rank // n_fy, rank % n_fy)

    def line_target(offset):
        place = lax.rem(my_high + offset, high)
        return (place * low + my_low, j)

    routes = [
        (1, i < n_fx - 1, (i + 1, j), i > 0),
        (0, i > 0, (i - 1, j), i < n_fx - 1),
        (3, j < n_fy - 1, (i, j + 1), j > 0),
        (2, j > 0, (i, j - 1), j < n_fy - 1),
    ]

    loads = [pltpu.make_async_copy(coupling_ref.at[k], stage.at[k], load_sem.at[k]) for k in range(BLOCKS)]
    for load in loads:
        load.start()

    barrier = pltpu.get_barrier_semaphore()
    for _, has_target, target, _ in routes:
        @pl.when(has_target)
        def _(target=target):
            pl.semaphore_signal(barrier, inc=1, device_id=target, device_id_type=MESH)
    for offset in range(1, plane):
        pl.semaphore_signal(barrier, inc=1, device_id=plane_target(offset)[1], device_id_type=MESH)
    for offset in range(1, high):
        pl.semaphore_signal(barrier, inc=1, device_id=line_target(offset), device_id_type=MESH)

    g8 = lane_group(8)
    g64 = lane_group(DOF)
    g32 = lane_group(HALF)

    for block in range(faces // 8):
        for tile in range(DOF // GROUPS):
            x = right_ref[8 * block:8 * block + 8, tile * LANES:(tile + 1) * LANES]
            moved = rolls(x)
            for q in range(GROUPS):
                wide[0, pl.ds(8 * block * DOF + tile * GROUPS + q, 8, stride=DOF), :] = replicate(g8, moved, q)
    for face in range(faces):
        w0[face] = wide[0, face * DOF:(face + 1) * DOF, :]

    def field_copies(power):
        return [
            pltpu.make_async_remote_copy(
                src_ref=send_buf.at[power, q], dst_ref=recv_buf.at[power, q],
                send_sem=send_sem.at[power, q], recv_sem=recv_sem.at[power, q],
                device_id=routes[q][2], device_id_type=MESH,
            )
            for q in range(4)
        ]

    def send_field(power):
        field = fields[power]
        copies = field_copies(power)
        for q, (row, has_target, _, _) in enumerate(routes):
            picked = [field[ghost_ref[row, g]] for g in range(GROUPS)]
            send_buf[power, q] = pick(g64, picked)
            if power == 0 and q == 0:
                count = sum(jnp.where(route[1], 1, 0) for route in routes) + (plane - 1) + (high - 1)
                pl.semaphore_wait(barrier, count)

            @pl.when(has_target)
            def _(copy=copies[q]):
                copy.start()
        return copies

    def build_own(power):
        field = fields[power]

        @pl.loop(0, faces, unroll=4)
        def _(face):
            x = field[face]
            top, bottom = product_tile(x, g64)
            tiles[face, 0:DOF] = top
            tiles[face, DOF:2 * DOF] = bottom

    def own_products():
        @pl.loop(0, faces // UNROLL)
        def _(part):
            for sub in range(UNROLL):
                face = part * UNROLL + sub
                right = jnp.concatenate([tiles[columns_ref[face, k]] for k in range(OWNED)], axis=0)
                out = jnp.dot(mats[face, :, :OWNED * LANES], right, preferred_element_type=f32)
                acc[face] = out[:HALF] + out[HALF:]

    def far_products(power):
        field = fields[power + 1]

        @pl.loop(0, faces // UNROLL)
        def _(part):
            for sub in range(UNROLL):
                face = part * UNROLL + sub
                right = jnp.concatenate(
                    [tiles[columns_ref[face, k]] for k in range(OWNED, BLOCKS)], axis=0
                )
                out = jnp.dot(mats[face, :, OWNED * LANES:], right, preferred_element_type=f32)
                total = acc[face] + (out[:HALF] + out[HALF:])
                total = total + pltpu.roll(total, LANES // 2, 1)
                turned = pltpu.roll(total, NRHS, 1)
                even = g32 % 2 == 0
                field[face, pl.ds(0, HALF, stride=2), :] = jnp.where(even, total, turned)
                field[face, pl.ds(1, HALF, stride=2), :] = jnp.where(even, turned, total)

    def receive_field(power, copies):
        for q in (2, 3, 0, 1):
            _, has_target, _, has_source = routes[q]

            @pl.when(has_source)
            def _(copy=copies[q]):
                copy.wait_recv()

            @pl.when(jnp.logical_not(has_source))
            def _(q=q):
                recv_buf[power, q] = jnp.zeros((DOF, LANES), f32)
            moved = rolls(recv_buf[power, q])
            for g in range(GROUPS):
                top, bottom = product_tile(replicate(g64, moved, g), g64)
                tiles[faces + q * GROUPS + g, 0:DOF] = top
                tiles[faces + q * GROUPS + g, DOF:2 * DOF] = bottom

            @pl.when(has_target)
            def _(copy=copies[q]):
                copy.wait_send()

    def prepare():
        for k in range(BLOCKS):
            loads[k].wait()
            for block in range(faces // 8):
                for t in range(HALF):
                    spread[k % 2, pl.ds(8 * block * HALF + t, 8, stride=HALF), :] = stage[
                        k, 8 * block:8 * block + 8, t * LANES:(t + 1) * LANES]
            for face in range(faces):
                hi, lo = split(spread[k % 2, face * HALF:(face + 1) * HALF, :])
                mats[face, 0:HALF, k * LANES:(k + 1) * LANES] = hi.astype(bf16)
                mats[face, HALF:DOF, k * LANES:(k + 1) * LANES] = lo.astype(bf16)

    for power in range(POWERS):
        copies = send_field(power)
        build_own(power)
        if power == 0:
            prepare()
        own_products()
        receive_field(power, copies)
        far_products(power)

    @pl.loop(0, faces, unroll=4)
    def _(face):
        rows = pl.ds(pl.multiple_of(face * DOF, DOF), DOF)
        a, b, c, d = [field[face] for field in fields]
        hi, lo = split(pick(g64, [a + b, b + c, c + d, a]))
        zbuf[rows, :LANES] = hi.astype(bf16)
        zbuf[rows, LANES:] = lo.astype(bf16)

    z = zbuf[...]
    both = lax.dot_general(z, z, (((0,), (0,)), ((), ())), preferred_element_type=f32)
    gram = (both[:LANES, :LANES] + both[LANES:, LANES:]) + (both[:LANES, LANES:] + both[LANES:, :LANES])
    share = LANES // plane
    for rank in range(plane):
        gram_buf[rank] = gram[rank * share:(rank + 1) * share]

    copies = []
    for offset in range(1, plane):
        rank, target = plane_target(offset)
        copy = pltpu.make_async_remote_copy(
            src_ref=gram_buf.at[rank], dst_ref=plane_recv.at[offset], send_sem=ps_sem.at[offset],
            recv_sem=pr_sem.at[offset], device_id=target, device_id_type=MESH)
        copy.start()
        copies.append(copy)

    @pl.loop(0, faces, unroll=4)
    def _(face):
        rows = pl.ds(pl.multiple_of(face * DOF, DOF), DOF)
        hi, lo = split(pick(g64, [field[face] for field in fields]))
        vbuf[rows, :LANES] = hi.astype(bf16)
        vbuf[rows, LANES:] = lo.astype(bf16)

    total = gram_buf[my_rank]
    for offset, copy in enumerate(copies, 1):
        copy.wait_recv()
        total = total + plane_recv[offset]
    line_recv[my_high] = total
    line = []
    for offset in range(1, high):
        copy = pltpu.make_async_remote_copy(
            src_ref=line_recv.at[my_high], dst_ref=line_recv.at[my_high], send_sem=ls_sem.at[offset],
            recv_sem=lr_sem.at[offset], device_id=line_target(offset), device_id_type=MESH)
        copy.start()
        line.append(copy)
    for copy in copies:
        copy.wait_send()
    for copy in line:
        copy.wait_recv()
    total = line_recv[0]
    for place in range(1, high):
        total = total + line_recv[place]
    final_buf[my_rank] = total
    gather = []
    for offset in range(1, plane):
        copy = pltpu.make_async_remote_copy(
            src_ref=final_buf.at[my_rank], dst_ref=final_buf.at[my_rank], send_sem=as_sem.at[offset],
            recv_sem=ar_sem.at[offset], device_id=plane_target(offset)[1], device_id_type=MESH)
        copy.start()
        gather.append(copy)
    for copy in line:
        copy.wait_send()
    for copy in gather:
        copy.wait_recv()

    full = jnp.concatenate([final_buf[rank] for rank in range(plane)], axis=0)
    count = POWERS * NRHS
    tiles = [full[8 * t:8 * t + 8] for t in range(count // 8)]
    sub = lax.broadcasted_iota(jnp.int32, (8, LANES), 0)

    def across(x, lane):
        return jnp.broadcast_to(x[:, lane:lane + 1], (8, LANES))

    def down(x, row):
        return jnp.broadcast_to(x[row:row + 1, :], (8, LANES))

    for home in range(len(tiles)):
        mine = tiles[home]
        cols = [across(mine, 8 * home + c) for c in range(8)]
        for step in range(8):
            inverse = 1.0 / down(cols[step], step)
            here = sub == step
            factor = cols[step]
            scaled = down(mine, step) * inverse
            mine = jnp.where(here, scaled, mine - factor * scaled)
            for c in range(step + 1, 8):
                scaled = down(cols[c], step) * inverse
                cols[c] = jnp.where(here, scaled, cols[c] - factor * scaled)
        tiles[home] = mine
        rows8 = [down(mine, c) for c in range(8)]
        order = [t % len(tiles) for t in range(home + 1, home + len(tiles))]
        for t in order:
            terms = [across(tiles[t], 8 * home + c) * rows8[c] for c in range(8)]
            while len(terms) > 1:
                terms = [terms[k] + terms[k + 1] for k in range(0, len(terms), 2)]
            tiles[t] = tiles[t] - terms[0]
    solved = jnp.concatenate(tiles, axis=0)
    coeffs = replicate(lane_group(count), rolls(solved), GROUPS - 1)
    none = jnp.zeros((NRHS, LANES), f32)
    row = lax.broadcasted_iota(jnp.int32, (LANES, LANES), 0)
    col = lax.broadcasted_iota(jnp.int32, (LANES, LANES), 1) % NRHS
    first = jnp.where(row == col, 1.0, 0.0)
    padded = jnp.concatenate([coeffs, none], axis=0)
    combo = first - (padded + jnp.concatenate([none, coeffs], axis=0))
    hi, lo = split(jnp.concatenate([padded, combo], axis=1))
    hi, lo = hi.astype(bf16), lo.astype(bf16)
    twice = jnp.concatenate([hi, hi], axis=0)

    @pl.loop(0, faces // 4, unroll=True)
    def _(quad):
        rows = pl.ds(pl.multiple_of(quad * 4 * DOF, 4 * DOF), 4 * DOF)
        left = vbuf[rows, :]
        out = jnp.dot(left, twice, preferred_element_type=f32)
        wide_part = out + jnp.dot(left[:, :LANES], lo, preferred_element_type=f32)
        wide[0, rows, :] = wide_part[:, :LANES]
        wide[1, rows, :] = wide_part[:, LANES:]
    for part, out_ref in enumerate((sol_ref, res_ref)):
        for block in range(faces // 8):
            for tile in range(DOF // GROUPS):
                parts = [
                    wide[part, pl.ds(8 * block * DOF + tile * GROUPS + q, 8, stride=DOF), :] for q in range(GROUPS)
                ]
                out_ref[8 * block:8 * block + 8, tile * LANES:(tile + 1) * LANES] = pick(g8, parts)
    for copy in gather:
        copy.wait_send()


def on_device(shape, right_side, coupling, face_columns, ghost_lists):
    n_fx, n_fy, low, faces = shape
    plane = low * n_fy
    high = n_fx // low
    share = LANES // plane
    rows = faces * DOF
    vmem = pl.BlockSpec(memory_space=pltpu.VMEM)
    smem = pl.BlockSpec(memory_space=pltpu.SMEM)
    dma = pltpu.SemaphoreType.DMA
    out = jax.ShapeDtypeStruct(right_side.shape, f32)
    return pl.pallas_call(
        functools.partial(kernel, shape),
        out_shape=(out, out),
        in_specs=[vmem, pl.BlockSpec(memory_space=pltpu.HBM), smem, smem],
        out_specs=(vmem, vmem),
        scratch_shapes=[
            pltpu.VMEM(coupling.shape, f32),
            pltpu.VMEM((2, faces * HALF, LANES), f32),
            pltpu.VMEM((faces, DOF, BLOCKS * LANES), bf16),
        ]
        + [pltpu.VMEM((faces, DOF, LANES), f32)] * (POWERS + 1)
        + [
            pltpu.VMEM((faces + 4 * GROUPS, LANES, LANES), bf16),
            pltpu.VMEM((faces, HALF, LANES), f32),
            pltpu.VMEM((POWERS, 4, DOF, LANES), f32),
            pltpu.VMEM((POWERS, 4, DOF, LANES), f32),
            pltpu.VMEM((rows, 2 * LANES), bf16),
            pltpu.VMEM((rows, 2 * LANES), bf16),
            pltpu.VMEM((plane, share, LANES), f32),
            pltpu.VMEM((plane, share, LANES), f32),
            pltpu.VMEM((high, share, LANES), f32),
            pltpu.VMEM((plane, share, LANES), f32),
            pltpu.VMEM((2, rows, LANES), f32),
            dma((BLOCKS,)),
            dma((POWERS, 4)),
            dma((POWERS, 4)),
            dma((plane,)),
            dma((plane,)),
            dma((high,)),
            dma((high,)),
            dma((plane,)),
            dma((plane,)),
        ],
        compiler_params=pltpu.CompilerParams(
            collective_id=0, has_side_effects=True, vmem_limit_bytes=40 * 2**20
        ),
    )(right_side, pltpu.with_memory_space_constraint(coupling, pltpu.HBM), face_columns, ghost_lists)


def solution(mesh):
    n_fx, n_fy = mesh.shape["fx"], mesh.shape["fy"]
    low = 1
    while low * low * 4 <= n_fx:
        low *= 2

    def body(right_side, coupling, face_columns, ghost_lists):
        shape = (n_fx, n_fy, low, right_side.shape[0])
        return on_device(shape, right_side, coupling.transpose(1, 0, 2), face_columns, ghost_lists)

    placed = (
        P(("fx", "fy"), None),
        P(("fx", "fy"), None, None),
        P(("fx", "fy"), None),
        P(("fx", "fy"), None),
    )
    return jax.shard_map(
        body,
        mesh=mesh,
        in_specs=placed,
        out_specs=(P(("fx", "fy"), None), P(("fx", "fy"), None)),
        check_vma=False,
    )
```

profile of v0, /device:TPU:0, one launch (start us, length us, event | category | flops | bytes accessed | tf_op | source)
XLA Modules:
  0.0 38.5 jit_solution(14966912380122649099)
XLA Ops:
  0.6 0.0 copy-start
  0.6 0.9 %copy-done = f32[16,2048]{1,0:T(8,128)S(1)} copy-done((f32[16,2048]{1,0:T(8,128)S(1)}, f32[16,2048]{1,0:T(8,128)}, u32[]{:S(2)}) %copy-start) | copy-done | bytes 131096
  1.5 0.0 copy-start.1
  1.5 0.7 %copy-done.1 = s32[16,11]{1,0:T(8,128)S(1)} copy-done((s32[16,11]{1,0:T(8,128)S(1)}, s32[16,11]{1,0:T(8,128)}, u32[]{:S(2)}) %copy-start.1) | copy-done | bytes 728
  2.2 0.0 copy-start.2
  2.2 0.7 %copy-done.2 = s32[4,4]{1,0:T(4,128)S(1)} copy-done((s32[4,4]{1,0:T(4,128)S(1)}, s32[4,4]{1,0:T(4,128)}, u32[]{:S(2)}) %copy-start.2) | copy-done | bytes 88
  2.9 34.3 %shard_map.59 = (f32[16,2048]{1,0:T(8,128)S(1)}, f32[16,2048]{1,0:T(8,128)S(1)}) custom-call(f32[16,2048]{1,0:T(8,128)S(1)} %copy-done, f32[11,16,4096]{2,1,0:T(8,128)} %bitcast.1, s32[16,11]{1,0:T(8,128)S(1)} %copy-done.1, s32[4,4]{1,0:T(4,128)S(1)} %copy-done.2), custom_call_target="tpu_custom_call" | custom-call | tf_op jit(solution)/shard_map/pallas_call | solution.py:351
  37.2 0.7 %copy.8 = f32[16,2048]{1,0:T(8,128)} copy(f32[16,2048]{1,0:T(8,128)S(1)} %get-tuple-element.4) | data formatting | bytes 262144
  37.8 0.7 %copy.9 = f32[16,2048]{1,0:T(8,128)} copy(f32[16,2048]{1,0:T(8,128)S(1)} %get-tuple-element.5) | data formatting | bytes 262144
Async XLA Ops:
  0.6 0.9 %copy-start = (f32[16,2048]{1,0:T(8,128)S(1)}, f32[16,2048]{1,0:T(8,128)}, u32[]{:S(2)}) copy-start(f32[16,2048]{1,0:T(8,128)} %right_ref.1) | copy-start | bytes 393220
  1.5 0.7 %copy-start.1 = (s32[16,11]{1,0:T(8,128)S(1)}, s32[16,11]{1,0:T(8,128)}, u32[]{:S(2)}) copy-start(s32[16,11]{1,0:T(8,128)} %columns_ref.1) | copy-start | bytes 2116
  2.2 0.7 %copy-start.2 = (s32[4,4]{1,0:T(4,128)S(1)}, s32[4,4]{1,0:T(4,128)}, u32[]{:S(2)}) copy-start(s32[4,4]{1,0:T(4,128)} %ghost_ref.1) | copy-start | bytes 196
where the time goes:
time: 38.7 us; the launch traced here: 38.5 us
  Pallas kernels  34.3 us (89%)
  local copies, waits for them, and re-layouts  3.59 us (9%)
  between operations  0.65 us (2%)
    pallas_call x1, Pallas kernels, on_device(): pl.pallas_call(functools.partial(kernel, shape), out_shape=(out, out), in...  34.3 us
    unnamed x8, local copies, waits for them, and re-layouts  3.59 us

commit v1 on v0

--- a/solution.py
+++ b/solution.py
@@ -53,10 +53,10 @@
     return top.astype(bf16), bottom.astype(bf16)
 
 
-def kernel(shape, right_ref, coupling_ref, columns_ref, ghost_ref, sol_ref, res_ref,
-           stage, spread, mats, w0, w1, w2, w3, tiles, acc, send_buf, recv_buf,
+def kernel(shape, right_hbm, coupling_ref, columns_hbm, ghost_hbm, sol_ref, res_ref,
+           right_ref, columns_ref, ghost_ref, stage, spread, mats, w0, w1, w2, w3, tiles, acc, send_buf, recv_buf,
            zbuf, vbuf, gram_buf, plane_recv, line_recv, final_buf, wide,
-           load_sem, send_sem, recv_sem, ps_sem, pr_sem, ls_sem, lr_sem, as_sem, ar_sem):
+           small_sem, load_sem, send_sem, recv_sem, ps_sem, pr_sem, ls_sem, lr_sem, as_sem, ar_sem):
     n_fx, n_fy, low, faces = shape
     plane = low * n_fy
     high = n_fx // low
@@ -82,6 +82,13 @@
         (2, j > 0, (i, j - 1), j < n_fy - 1),
     ]
 
+    small = [
+        pltpu.make_async_copy(right_hbm, right_ref, small_sem.at[0]),
+        pltpu.make_async_copy(ghost_hbm, ghost_ref, small_sem.at[1]),
+        pltpu.make_async_copy(columns_hbm, columns_ref, small_sem.at[2]),
+    ]
+    for load in small:
+        load.start()
     loads = [pltpu.make_async_copy(coupling_ref.at[k], stage.at[k], load_sem.at[k]) for k in range(BLOCKS)]
     for load in loads:
         load.start()
@@ -100,6 +107,7 @@
     g64 = lane_group(DOF)
     g32 = lane_group(HALF)
 
+    small[0].wait()
     for block in range(faces // 8):
         for tile in range(DOF // GROUPS):
             x = right_ref[8 * block:8 * block + 8, tile * LANES:(tile + 1) * LANES]
@@ -108,6 +116,9 @@
                 wide[0, pl.ds(8 * block * DOF + tile * GROUPS + q, 8, stride=DOF), :] = replicate(g8, moved, q)
     for face in range(faces):
         w0[face] = wide[0, face * DOF:(face + 1) * DOF, :]
+
+    small[1].wait()
+    small[2].wait()
 
     def field_copies(power):
         return [
@@ -345,15 +356,18 @@
     share = LANES // plane
     rows = faces * DOF
     vmem = pl.BlockSpec(memory_space=pltpu.VMEM)
-    smem = pl.BlockSpec(memory_space=pltpu.SMEM)
+    hbm = pl.BlockSpec(memory_space=pltpu.HBM)
     dma = pltpu.SemaphoreType.DMA
     out = jax.ShapeDtypeStruct(right_side.shape, f32)
     return pl.pallas_call(
         functools.partial(kernel, shape),
         out_shape=(out, out),
-        in_specs=[vmem, pl.BlockSpec(memory_space=pltpu.HBM), smem, smem],
+        in_specs=[hbm] * 4,
         out_specs=(vmem, vmem),
         scratch_shapes=[
+            pltpu.VMEM(right_side.shape, f32),
+            pltpu.SMEM(face_columns.shape, jnp.int32),
+            pltpu.SMEM(ghost_lists.shape, jnp.int32),
             pltpu.VMEM(coupling.shape, f32),
             pltpu.VMEM((2, faces * HALF, LANES), f32),
             pltpu.VMEM((faces, DOF, BLOCKS * LANES), bf16),
@@ -371,6 +385,7 @@
             pltpu.VMEM((high, share, LANES), f32),
             pltpu.VMEM((plane, share, LANES), f32),
             pltpu.VMEM((2, rows, LANES), f32),
+            dma((3,)),
             dma((BLOCKS,)),
             dma((POWERS, 4)),
             dma((POWERS, 4)),
@@ -384,7 +399,7 @@
         compiler_params=pltpu.CompilerParams(
             collective_id=0, has_side_effects=True, vmem_limit_bytes=40 * 2**20
         ),
-    )(right_side, pltpu.with_memory_space_constraint(coupling, pltpu.HBM), face_columns, ghost_lists)
+    )(*[pltpu.with_memory_space_constraint(x, pltpu.HBM) for x in (right_side, coupling, face_columns, ghost_lists)])
 
 
 def solution(mesh):

time: 38.7 us -> 35.7 us (0.922)
  local copies, waits for them, and re-layouts: 3.59 us -> 1.31 us
  Pallas kernels: 34.3 us -> 33.6 us
    unnamed x8 -> x2, local copies, waits for them, and re-layouts: 3.59 us -> 1.31 us
    pallas_call x1, Pallas kernels: 34.3 us -> 33.6 us  [on_device(): pl.pallas_call(functools.partial(kernel, shape), out_shape=(out, out), in...]
where the time goes in v1:
time: 35.7 us; the launch traced here: 35.6 us
  Pallas kernels  33.6 us (94%)
  local copies, waits for them, and re-layouts  1.31 us (4%)
  between operations  0.64 us (2%)
    pallas_call x1, Pallas kernels, on_device(): pl.pallas_call(functools.partial(kernel, shape), out_shape=(out, out), in...  33.6 us
    unnamed x2, local copies, waits for them, and re-layouts  1.31 us

profile of v1, /device:TPU:0, one launch (start us, length us, event | category | flops | bytes accessed | tf_op | source)
XLA Modules:
  0.0 35.6 jit_solution(14626276674684542319)
XLA Ops:
  0.6 33.6 %shard_map.59 = (f32[16,2048]{1,0:T(8,128)S(1)}, f32[16,2048]{1,0:T(8,128)S(1)}) custom-call(f32[16,2048]{1,0:T(8,128)} %right_hbm.1, f32[11,16,4096]{2,1,0:T(8,128)} %bitcast.1, s32[16,11]{1,0:T(8,128)} %columns_hbm.1, s32[4,4]{1,0:T(4,128)} %ghost_hbm.1), custom_call_target="tpu_custom_call" | custom-call | tf_op jit(solution)/shard_map/pallas_call | solution.py:362
  34.3 0.7 %copy.8 = f32[16,2048]{1,0:T(8,128)} copy(f32[16,2048]{1,0:T(8,128)S(1)} %get-tuple-element.4) | data formatting | bytes 262144
  34.9 0.7 %copy.9 = f32[16,2048]{1,0:T(8,128)} copy(f32[16,2048]{1,0:T(8,128)S(1)} %get-tuple-element.5) | data formatting | bytes 262144

commit v2 on v1

v2 whole, which is shorter than its diff:
```python
import contextlib
import functools

import jax
import jax.numpy as jnp
from jax import lax
from jax.experimental import pallas as pl
from jax.experimental.pallas import tpu as pltpu
from jax.sharding import PartitionSpec as P

DOF = 64
NRHS = 32
BLOCKS = 11
OWNED = 7
POWERS = 3
LANES = 128
HALF = DOF // 2
BATCH = 3
GROUPS = LANES // NRHS
MESH = pl.DeviceIdType.MESH
f32 = jnp.float32
bf16 = jnp.bfloat16


def split(x):
    hi = x.astype(bf16).astype(f32)
    return hi, x - hi


def lane_group(rows):
    return lax.broadcasted_iota(jnp.int32, (rows, LANES), 1) // NRHS


def pick(group, parts):
    out = parts[-1]
    for index in range(len(parts) - 2, -1, -1):
        out = jnp.where(group == index, parts[index], out)
    return out


def replicate(group, rolled, source):
    return pick(group, [rolled[(lane - source) % GROUPS] for lane in range(GROUPS)])


def rolls(x):
    return [x] + [pltpu.roll(x, step * NRHS, 1) for step in range(1, GROUPS)]


def product_tile(x, group):
    hi, lo = split(x)
    zero = jnp.zeros_like(x)
    top = pick(group, [hi, zero, lo, zero])
    bottom = pick(group, [zero, hi, zero, lo])
    return top.astype(bf16), bottom.astype(bf16)


def scope(name):
    return contextlib.nullcontext()


def eliminate(tiles, inverse):
    tiles = list(tiles)
    sub = lax.broadcasted_iota(jnp.int32, (8, LANES), 0)
    lanes = lax.broadcasted_iota(jnp.int32, (8, LANES), 1)

    def across(x, lane):
        return jnp.broadcast_to(x[:, lane:lane + 1], (8, LANES))

    def down(x, row):
        return jnp.broadcast_to(x[row:row + 1, :], (8, LANES))

    for home in range(len(tiles)):
        mine = tiles[home]
        cols = [across(mine, 8 * home + c) for c in range(8)]
        for step in range(8):
            pivot = 1.0 / down(cols[step], step)
            here = sub == step
            factor = cols[step]
            if inverse:
                mine = jnp.where(lanes == 8 * home + step, jnp.where(here, 1.0, 0.0), mine)
            scaled = down(mine, step) * pivot
            mine = jnp.where(here, scaled, mine - factor * scaled)
            for c in range(step + 1, 8):
                scaled = down(cols[c], step) * pivot
                cols[c] = jnp.where(here, scaled, cols[c] - factor * scaled)
        tiles[home] = mine
        rows8 = [down(mine, c) for c in range(8)]
        for t in [t % len(tiles) for t in range(home + 1, home + len(tiles))]:
            terms = [across(tiles[t], 8 * home + c) * rows8[c] for c in range(8)]
            while len(terms) > 1:
                terms = [terms[k] + terms[k + 1] for k in range(0, len(terms), 2)]
            base = jnp.where(lanes // 8 == home, 0.0, tiles[t]) if inverse else tiles[t]
            tiles[t] = base - terms[0]
    return jnp.concatenate(tiles, axis=0)


def high_dot(left, right, dims):
    return lax.dot_general(left, right, (dims, ((), ())), precision=lax.Precision.HIGHEST, preferred_element_type=f32)


def kernel(shape, right_hbm, coupling_hbm, columns_hbm, ghost_hbm, sol_ref, res_ref,
           right_ref, columns_ref, ghost_ref,
           stage, spread, mats, w0, w1, w2, w3, tiles, acc, send_buf, recv_buf,
           zbuf, newest, vbuf, early_buf, early_plane, early_line, early_all,
           late_buf, late_plane, late_line, late_all, wide,
           small_sem, load_sem, send_sem, recv_sem, gram_sem):
    n_fx, n_fy, low, faces = shape
    plane = low * n_fy
    high = n_fx // low
    i = lax.axis_index("fx")
    j = lax.axis_index("fy")
    my_low = i % low
    my_high = i // low
    my_rank = my_low * n_fy + j
    fields = [w0, w1, w2, w3]

    def plane_target(offset):
        rank = lax.rem(my_rank + offset, plane)
        return rank, (my_high * low + rank // n_fy, rank % n_fy)

    def line_target(offset):
        place = lax.rem(my_high + offset, high)
        return (place * low + my_low, j)

    routes = [
        (1, i < n_fx - 1, (i + 1, j), i > 0),
        (0, i > 0, (i - 1, j), i < n_fx - 1),
        (3, j < n_fy - 1, (i, j + 1), j > 0),
        (2, j > 0, (i, j - 1), j < n_fy - 1),
    ]

    small = [
        pltpu.make_async_copy(src, dst, small_sem.at[place])
        for place, (src, dst) in enumerate([
            (right_hbm, right_ref), (ghost_hbm, ghost_ref), (columns_hbm, columns_ref),
        ])
    ]
    for load in small:
        load.start()
    batches = [(k, min(k + BATCH, BLOCKS)) for k in range(0, BLOCKS, BATCH)]
    loads = [
        pltpu.make_async_copy(coupling_hbm.at[first:last], stage.at[first:last], load_sem.at[place])
        for place, (first, last) in enumerate(batches)
    ]
    for load in loads:
        load.start()

    barrier = pltpu.get_barrier_semaphore()
    for _, has_target, target, _ in routes:
        @pl.when(has_target)
        def _(target=target):
            pl.semaphore_signal(barrier, inc=1, device_id=target, device_id_type=MESH)
    for offset in range(1, plane):
        pl.semaphore_signal(barrier, inc=1, device_id=plane_target(offset)[1], device_id_type=MESH)
    for offset in range(1, high):
        pl.semaphore_signal(barrier, inc=1, device_id=line_target(offset), device_id_type=MESH)

    g8 = lane_group(8)
    g64 = lane_group(DOF)
    g32 = lane_group(HALF)

    with scope("relay"):
        small[0].wait()
        for block in range(faces // 8):
            for tile in range(DOF // GROUPS):
                x = right_ref[8 * block:8 * block + 8, tile * LANES:(tile + 1) * LANES]
                moved = rolls(x)
                for q in range(GROUPS):
                    wide[pl.ds(8 * block * DOF + tile * GROUPS + q, 8, stride=DOF), :] = replicate(g8, moved, q)
        for face in range(faces):
            w0[face] = wide[face * DOF:(face + 1) * DOF, :]
        small[1].wait()

    def field_copies(power):
        return [
            pltpu.make_async_remote_copy(
                src_ref=send_buf.at[power, q], dst_ref=recv_buf.at[power, q],
                send_sem=send_sem.at[q], recv_sem=recv_sem.at[power % 2, q],
                device_id=routes[q][2], device_id_type=MESH,
            )
            for q in range(4)
        ]

    def send_field(power):
        field = fields[power]
        copies = field_copies(power)
        for q, (row, _, _, _) in enumerate(routes):
            picked = [field[ghost_ref[row, g]] for g in range(GROUPS)]
            send_buf[power, q] = pick(g64, picked)
        if power == 0:
            count = sum(jnp.where(route[1], 1, 0) for route in routes) + (plane - 1) + (high - 1)
            pl.semaphore_wait(barrier, count)
        far_down = my_low == 0
        starts = [
            (1, jnp.logical_and(routes[1][1], far_down)),
            (0, routes[0][1]),
            (1, jnp.logical_and(routes[1][1], jnp.logical_not(far_down))),
            (2, routes[2][1]),
            (3, routes[3][1]),
        ]
        for q, needed in starts:
            @pl.when(needed)
            def _(copy=copies[q]):
                copy.start()
        return copies

    def build_own(power):
        field = fields[power]

        @pl.loop(0, faces, unroll=4)
        def _(face):
            x = field[face]
            top, bottom = product_tile(x, g64)
            tiles[face, 0:DOF] = top
            tiles[face, DOF:2 * DOF] = bottom

    def own_products():
        for face in range(faces):
            left = jnp.concatenate([mats[face * BLOCKS + k] for k in range(OWNED)], axis=1)
            right = jnp.concatenate([tiles[columns_ref[face, k]] for k in range(OWNED)], axis=0)
            out = jnp.dot(left, right, preferred_element_type=f32)
            acc[face] = out[:HALF] + out[HALF:]

    def far_products(power):
        field = fields[power + 1]
        for face in range(faces):
            left = jnp.concatenate([mats[face * BLOCKS + k] for k in range(OWNED, BLOCKS)], axis=1)
            right = jnp.concatenate([tiles[columns_ref[face, k]] for k in range(OWNED, BLOCKS)], axis=0)
            out = jnp.dot(left, right, preferred_element_type=f32)
            total = acc[face] + (out[:HALF] + out[HALF:])
            total = total + pltpu.roll(total, LANES // 2, 1)
            turned = pltpu.roll(total, NRHS, 1)
            even = g32 % 2 == 0
            field[face, pl.ds(0, HALF, stride=2), :] = jnp.where(even, total, turned)
            field[face, pl.ds(1, HALF, stride=2), :] = jnp.where(even, turned, total)

    def receive_field(power, copies):
        for q in (2, 3, 0, 1):
            _, has_target, _, has_source = routes[q]

            with scope("recv%d_%d" % (power, q)):
                @pl.when(has_source)
                def _(copy=copies[q]):
                    copy.wait_recv()

                @pl.when(jnp.logical_not(has_source))
                def _(q=q):
                    recv_buf[power, q] = jnp.zeros((DOF, LANES), f32)
            with scope("conv%d_%d" % (power, q)):
                moved = rolls(recv_buf[power, q])
                for g in range(GROUPS):
                    top, bottom = product_tile(replicate(g64, moved, g), g64)
                    tiles[faces + q * GROUPS + g, 0:DOF] = top
                    tiles[faces + q * GROUPS + g, DOF:2 * DOF] = bottom

            @pl.when(has_target)
            def _(copy=copies[q]):
                copy.wait_send()

    def prepare():
        for k in range(BLOCKS):
            for place, (first, _) in enumerate(batches):
                if first == k:
                    loads[place].wait()
            for block in range(faces // 8):
                for t in range(HALF):
                    spread[k % 2, pl.ds(8 * block * HALF + t, 8, stride=HALF), :] = stage[
                        k, 8 * block:8 * block + 8, t * LANES:(t + 1) * LANES]
            for face in range(faces):
                hi, lo = split(spread[k % 2, face * HALF:(face + 1) * HALF, :])
                mats[face * BLOCKS + k, 0:HALF] = hi.astype(bf16)
                mats[face * BLOCKS + k, HALF:DOF] = lo.astype(bf16)

    def wait_for(buf, count, sem):
        whole = buf.at[0:count]
        pltpu.make_async_copy(whole, whole, sem).wait()

    def scatter(which, buf, landed):
        for offset in range(1, plane):
            rank, target = plane_target(offset)
            pltpu.make_async_remote_copy(
                src_ref=buf.at[rank], dst_ref=landed.at[offset - 1], send_sem=gram_sem.at[which, 0],
                recv_sem=gram_sem.at[which, 1], device_id=target, device_id_type=MESH).start()

    def scatter_sum(which, buf, landed):
        total = buf[my_rank]
        wait_for(landed, plane - 1, gram_sem.at[which, 1])
        for offset in range(1, plane):
            total = total + landed[offset - 1]
        return total

    def exchange(which, line, total):
        line[my_high] = total
        for offset in range(1, high):
            pltpu.make_async_remote_copy(
                src_ref=line.at[my_high], dst_ref=line.at[my_high], send_sem=gram_sem.at[which, 2],
                recv_sem=gram_sem.at[which, 3], device_id=line_target(offset), device_id_type=MESH).start()

    def exchange_sum(which, line):
        wait_for(line, high - 1, gram_sem.at[which, 3])
        total = line[0]
        for place in range(1, high):
            total = total + line[place]
        return total

    def gather(which, final, total):
        final[my_rank] = total
        for offset in range(1, plane):
            pltpu.make_async_remote_copy(
                src_ref=final.at[my_rank], dst_ref=final.at[my_rank], send_sem=gram_sem.at[which, 4],
                recv_sem=gram_sem.at[which, 5], device_id=plane_target(offset)[1], device_id_type=MESH).start()

    def gathered(which, final):
        wait_for(final, plane - 1, gram_sem.at[which, 5])
        return jnp.concatenate([final[rank] for rank in range(plane)], axis=0)

    def early_gram():
        @pl.loop(0, faces, unroll=4)
        def _(face):
            rows = pl.ds(pl.multiple_of(face * DOF, DOF), DOF)
            a, b, c = w0[face], w1[face], w2[face]
            hi, lo = split(pick(g64, [a + b, b + c, jnp.zeros_like(a), a]))
            zbuf[rows, :LANES] = hi.astype(bf16)
            zbuf[rows, LANES:] = lo.astype(bf16)

        z = zbuf[...]
        both = lax.dot_general(z, z, (((0,), (0,)), ((), ())), preferred_element_type=f32)
        gram = (both[:LANES, :LANES] + both[LANES:, LANES:]) + (both[:LANES, LANES:] + both[LANES:, :LANES])
        share = early_buf.shape[1]
        for rank in range(plane):
            early_buf[rank] = gram[rank * share:(rank + 1) * share]

    def late_gram():
        @pl.loop(0, faces, unroll=4)
        def _(face):
            rows = pl.ds(pl.multiple_of(face * DOF, DOF), DOF)
            hi, lo = split(w2[face] + w3[face])
            zero = jnp.zeros_like(hi)
            zbuf[rows, :LANES] = zbuf[rows, :LANES] + pick(g64, [zero, zero, hi, zero]).astype(bf16)
            zbuf[rows, LANES:] = zbuf[rows, LANES:] + pick(g64, [zero, zero, lo, zero]).astype(bf16)
            newest[rows, :] = pick(g64, [hi, lo, zero, zero]).astype(bf16)

        both = lax.dot_general(newest[...], zbuf[...], (((0,), (0,)), ((), ())), preferred_element_type=f32)
        gram = (both[:NRHS, :LANES] + both[NRHS:2 * NRHS, LANES:]) + (both[:NRHS, LANES:] + both[NRHS:2 * NRHS, :LANES])
        share = late_buf.shape[1]
        for rank in range(plane):
            late_buf[rank] = gram[rank * share:(rank + 1) * share]

    flat = [field.reshape(faces * DOF, LANES) for field in fields]

    def order_rows():
        for block in range(faces // 8):
            for pair in range(DOF // GROUPS // 2):
                for q in range(GROUPS):
                    halves = []
                    for tile in (2 * pair, 2 * pair + 1):
                        at = pl.ds(8 * block * DOF + tile * GROUPS + q, 8, stride=DOF)
                        halves.append(pick(g8, [view[at, :] for view in flat]))
                    hi, lo = split(jnp.concatenate(halves, axis=0))
                    row = 8 * (block * (DOF // GROUPS) + 2 * pair)
                    vbuf[q, row:row + 16, :LANES] = hi.astype(bf16)
                    vbuf[q, row:row + 16, LANES:] = lo.astype(bf16)

    for power in range(POWERS):
        with scope("send%d" % power):
            copies = send_field(power)
        with scope("build%d" % power):
            build_own(power)
        if power == 0:
            with scope("prepare"):
                prepare()
                small[2].wait()
        if power == POWERS - 1:
            with scope("egram"):
                early_gram()
                scatter(0, early_buf, early_plane)
        with scope("own%d" % power):
            own_products()
        receive_field(power, copies)
        with scope("far%d" % power):
            far_products(power)

    with scope("lgram"):
        late_gram()
        scatter(1, late_buf, late_plane)
    with scope("eplane"):
        exchange(0, early_line, scatter_sum(0, early_buf, early_plane))
    with scope("order"):
        order_rows()
    with scope("lplane"):
        exchange(1, late_line, scatter_sum(1, late_buf, late_plane))
    with scope("eline"):
        gather(0, early_all, exchange_sum(0, early_line))
    with scope("lline"):
        gather(1, late_all, exchange_sum(1, late_line))
    with scope("eall"):
        system = gathered(0, early_all)
    with scope("esolve"):
        count = 2 * NRHS
        solved = eliminate([system[t:t + 8] for t in range(0, count, 8)], True)
        spread_early = replicate(lane_group(count), rolls(solved), GROUPS - 1)
    with scope("lall"):
        last = gathered(1, late_all)
    with scope("lsolve"):
        left_half = lax.broadcasted_iota(jnp.int32, (NRHS, LANES), 1) < count
        cross = jnp.where(left_half, last, 0.0)
        pad = jnp.zeros((LANES - count, LANES), f32)
        done = high_dot(cross, jnp.concatenate([solved, pad], axis=0), ((1,), (0,)))
        inner = jnp.where(left_half, done, 0.0)
        schur = high_dot(inner, jnp.concatenate([cross, jnp.zeros((LANES - NRHS, LANES), f32)], axis=0), ((1,), (1,)))
        small_system = pltpu.roll(jnp.where(left_half, 0.0, last - done), LANES // 2, 1) - schur
        newest_part = eliminate([small_system[t:t + 8] for t in range(0, NRHS, 8)], False)
        newest_part = replicate(g32, rolls(newest_part), 1)
        older = spread_early - high_dot(inner, newest_part, ((0,), (0,)))[:count]
        coeffs = jnp.concatenate([older, newest_part], axis=0)
    with scope("coeffs"):
        none = jnp.zeros((NRHS, LANES), f32)
        row = lax.broadcasted_iota(jnp.int32, (LANES, LANES), 0)
        col = lax.broadcasted_iota(jnp.int32, (LANES, LANES), 1) % NRHS
        first = jnp.where(row == col, 1.0, 0.0)
        padded = jnp.concatenate([coeffs, none], axis=0)
        combo = first - (padded + jnp.concatenate([none, coeffs], axis=0))
        hi, lo = split(jnp.concatenate([padded, combo], axis=1))
        group = lax.broadcasted_iota(jnp.int32, (LANES, 2 * LANES), 1) % LANES // NRHS
        his = [jnp.where(group == q, hi, 0.0).astype(bf16) for q in range(GROUPS)]
        los = [jnp.where(group == q, lo, 0.0).astype(bf16) for q in range(GROUPS)]
        right = jnp.concatenate(his + his + los, axis=0)
    with scope("outdot"):
        vhi = [vbuf[q, :, :LANES] for q in range(GROUPS)]
        vlo = [vbuf[q, :, LANES:] for q in range(GROUPS)]
        out = jnp.dot(jnp.concatenate(vhi + vlo + vhi, axis=1), right, preferred_element_type=f32)
        for part, out_ref in enumerate((sol_ref, res_ref)):
            for block in range(faces // 8):
                for tile in range(DOF // GROUPS):
                    row = 8 * (block * (DOF // GROUPS) + tile)
                    out_ref[8 * block:8 * block + 8, tile * LANES:(tile + 1) * LANES] = out[
                        row:row + 8, part * LANES:(part + 1) * LANES]
    with scope("drain"):
        for which, bufs in enumerate([(early_plane, early_line, early_all), (late_plane, late_line, late_all)]):
            for phase, (buf, amount) in enumerate(zip(bufs, (plane - 1, high - 1, plane - 1))):
                wait_for(buf, amount, gram_sem.at[which, 2 * phase])


def on_device(shape, right_side, coupling, face_columns, ghost_lists):
    n_fx, n_fy, low, faces = shape
    plane = low * n_fy
    high = n_fx // low
    rows = faces * DOF
    early = 2 * NRHS // plane
    late = NRHS // plane
    vmem = pl.BlockSpec(memory_space=pltpu.VMEM)
    hbm = pl.BlockSpec(memory_space=pltpu.HBM)
    dma = pltpu.SemaphoreType.DMA
    i32 = jnp.int32
    out = jax.ShapeDtypeStruct(right_side.shape, f32)
    gram = []
    for share in (early, late):
        gram += [
            pltpu.VMEM((plane, share, LANES), f32),
            pltpu.VMEM((plane - 1, share, LANES), f32),
            pltpu.VMEM((high, share, LANES), f32),
            pltpu.VMEM((plane, share, LANES), f32),
        ]
    return pl.pallas_call(
        functools.partial(kernel, shape),
        out_shape=(out, out),
        in_specs=[hbm] * 4,
        out_specs=(vmem, vmem),
        scratch_shapes=[
            pltpu.VMEM(right_side.shape, f32),
            pltpu.SMEM(face_columns.shape, i32),
            pltpu.SMEM(ghost_lists.shape, i32),
            pltpu.VMEM(coupling.shape, f32),
            pltpu.VMEM((2, faces * HALF, LANES), f32),
            pltpu.VMEM((faces * BLOCKS, DOF, LANES), bf16),
        ]
        + [pltpu.VMEM((faces, DOF, LANES), f32)] * (POWERS + 1)
        + [
            pltpu.VMEM((faces + 4 * GROUPS, LANES, LANES), bf16),
            pltpu.VMEM((faces, HALF, LANES), f32),
            pltpu.VMEM((POWERS, 4, DOF, LANES), f32),
            pltpu.VMEM((POWERS, 4, DOF, LANES), f32),
            pltpu.VMEM((rows, 2 * LANES), bf16),
            pltpu.VMEM((rows, LANES), bf16),
            pltpu.VMEM((GROUPS, rows // GROUPS, 2 * LANES), bf16),
        ]
        + gram
        + [
            pltpu.VMEM((rows, LANES), f32),
            dma((3,)),
            dma((-(-BLOCKS // BATCH),)),
            dma((4,)),
            dma((2, 4)),
            dma((2, 6)),
        ],
        compiler_params=pltpu.CompilerParams(
            collective_id=0, has_side_effects=True, vmem_limit_bytes=40 * 2**20
        ),
    )(*[pltpu.with_memory_space_constraint(x, pltpu.HBM) for x in (right_side, coupling, face_columns, ghost_lists)])


def solution(mesh):
    n_fx, n_fy = mesh.shape["fx"], mesh.shape["fy"]
    low = 1
    while low * low * 4 <= n_fx:
        low *= 2

    def body(right_side, coupling, face_columns, ghost_lists):
        shape = (n_fx, n_fy, low, right_side.shape[0])
        return on_device(shape, right_side, coupling.transpose(1, 0, 2), face_columns, ghost_lists)

    placed = (
        P(("fx", "fy"), None),
        P(("fx", "fy"), None, None),
        P(("fx", "fy"), None),
        P(("fx", "fy"), None),
    )
    return jax.shard_map(
        body,
        mesh=mesh,
        in_specs=placed,
        out_specs=(P(("fx", "fy"), None), P(("fx", "fy"), None)),
        check_vma=False,
    )
```

time: 35.7 us -> 33.3 us (0.933)
  Pallas kernels: 33.6 us -> 31.2 us
    pallas_call x1, Pallas kernels: 33.6 us -> 31.2 us  [on_device(): pl.pallas_call(functools.partial(kernel, shape), out_shape=(out, out), in...]
where the time goes in v2:
time: 33.3 us; the launch traced here: 33.1 us
  Pallas kernels  31.2 us (94%)
  local copies, waits for them, and re-layouts  1.31 us (4%)
  between operations  0.64 us (2%)
    pallas_call x1, Pallas kernels, on_device(): pl.pallas_call(functools.partial(kernel, shape), out_shape=(out, out), in...  31.2 us
    unnamed x2, local copies, waits for them, and re-layouts  1.31 us

profile of v2, /device:TPU:0, one launch (start us, length us, event | category | flops | bytes accessed | tf_op | source)
XLA Modules:
  0.0 33.1 jit_solution(411381024532780146)
XLA Ops:
  0.6 31.2 %shard_map.59 = (f32[16,2048]{1,0:T(8,128)S(1)}, f32[16,2048]{1,0:T(8,128)S(1)}) custom-call(f32[16,2048]{1,0:T(8,128)} %right_hbm.1, f32[11,16,4096]{2,1,0:T(8,128)} %bitcast.1, s32[16,11]{1,0:T(8,128)} %columns_hbm.1, s32[4,4]{1,0:T(4,128)} %ghost_hbm.1), custom_call_target="tpu_custom_call" | custom-call | tf_op jit(solution)/shard_map/pallas_call | solution.py:464
  31.8 0.7 %copy.8 = f32[16,2048]{1,0:T(8,128)} copy(f32[16,2048]{1,0:T(8,128)S(1)} %get-tuple-element.4) | data formatting | bytes 262144
  32.5 0.7 %copy.9 = f32[16,2048]{1,0:T(8,128)} copy(f32[16,2048]{1,0:T(8,128)S(1)} %get-tuple-element.5) | data formatting | bytes 262144

commit v3 on v2

--- a/solution.py
+++ b/solution.py
@@ -16,6 +16,7 @@
 LANES = 128
 HALF = DOF // 2
 BATCH = 3
+TOKENS = 2 * (POWERS - 1)
 GROUPS = LANES // NRHS
 MESH = pl.DeviceIdType.MESH
 f32 = jnp.float32
@@ -59,7 +60,6 @@
 
 
 def eliminate(tiles, inverse):
-    tiles = list(tiles)
     sub = lax.broadcasted_iota(jnp.int32, (8, LANES), 0)
     lanes = lax.broadcasted_iota(jnp.int32, (8, LANES), 1)
 
@@ -68,21 +68,33 @@
 
     def down(x, row):
         return jnp.broadcast_to(x[row:row + 1, :], (8, LANES))
+
+    scales = []
+    for home, tile in enumerate(tiles):
+        diagonal = jnp.sum(jnp.where(lanes == 8 * home + sub, tile, 0.0), axis=1, keepdims=True)
+        scales.append(1.0 / jnp.broadcast_to(diagonal, (8, LANES)))
+    tiles = [tile * scale for tile, scale in zip(tiles, scales)]
 
     for home in range(len(tiles)):
         mine = tiles[home]
         cols = [across(mine, 8 * home + c) for c in range(8)]
-        for step in range(8):
-            pivot = 1.0 / down(cols[step], step)
-            here = sub == step
-            factor = cols[step]
+        for p in range(0, 8, 2):
+            q = p + 1
+            left, right = cols[p], cols[q]
+            a, b, c, d = down(left, p), down(right, p), down(left, q), down(right, q)
+            pivot = 1.0 / (a * d - b * c)
+
+            def update(x):
+                top, bottom = down(x, p), down(x, q)
+                top, bottom = d * top - b * bottom, a * bottom - c * top
+                rest = x - pivot * (left * top + right * bottom)
+                return jnp.where(sub == p, pivot * top, jnp.where(sub == q, pivot * bottom, rest))
+
             if inverse:
-                mine = jnp.where(lanes == 8 * home + step, jnp.where(here, 1.0, 0.0), mine)
-            scaled = down(mine, step) * pivot
-            mine = jnp.where(here, scaled, mine - factor * scaled)
-            for c in range(step + 1, 8):
-                scaled = down(cols[c], step) * pivot
-                cols[c] = jnp.where(here, scaled, cols[c] - factor * scaled)
+                own = jnp.where(lanes == 8 * home + sub, scales[home], 0.0)
+                mine = jnp.where((lanes == 8 * home + p) | (lanes == 8 * home + q), jnp.where((sub == p) | (sub == q), own, 0.0), mine)
+            mine = update(mine)
+            cols = [update(x) if place > q else x for place, x in enumerate(cols)]
         tiles[home] = mine
         rows8 = [down(mine, c) for c in range(8)]
         for t in [t % len(tiles) for t in range(home + 1, home + len(tiles))]:
@@ -100,10 +112,10 @@
 
 def kernel(shape, right_hbm, coupling_hbm, columns_hbm, ghost_hbm, sol_ref, res_ref,
            right_ref, columns_ref, ghost_ref,
-           stage, spread, mats, w0, w1, w2, w3, tiles, acc, send_buf, recv_buf,
+           stage, mats, w0, w1, w2, w3, tiles, acc, send_buf, recv_buf,
            zbuf, newest, vbuf, early_buf, early_plane, early_line, early_all,
-           late_buf, late_plane, late_line, late_all, wide,
-           small_sem, load_sem, send_sem, recv_sem, gram_sem):
+           late_plane, late_line,
+           small_sem, load_sem, send_sem, recv_sem, gram_sem, token_sem):
     n_fx, n_fy, low, faces = shape
     plane = low * n_fy
     high = n_fx // low
@@ -132,44 +144,70 @@
     small = [
         pltpu.make_async_copy(src, dst, small_sem.at[place])
         for place, (src, dst) in enumerate([
-            (right_hbm, right_ref), (ghost_hbm, ghost_ref), (columns_hbm, columns_ref),
+            (ghost_hbm, ghost_ref), (columns_hbm, columns_ref),
         ])
     ]
-    for load in small:
+    rights = [
+        pltpu.make_async_copy(right_hbm.at[:, :, s], right_ref.at[:, s], small_sem.at[2]) for s in range(8)
+    ]
+    for load in rights + small:
         load.start()
     batches = [(k, min(k + BATCH, BLOCKS)) for k in range(0, BLOCKS, BATCH)]
     loads = [
-        pltpu.make_async_copy(coupling_hbm.at[first:last], stage.at[first:last], load_sem.at[place])
+        [
+            pltpu.make_async_copy(coupling_hbm.at[k, :, :, s], stage.at[k, :, s], load_sem.at[place])
+            for k in range(first, last) for s in range(8)
+        ]
         for place, (first, last) in enumerate(batches)
     ]
-    for load in loads:
-        load.start()
-
     barrier = pltpu.get_barrier_semaphore()
     for _, has_target, target, _ in routes:
         @pl.when(has_target)
         def _(target=target):
             pl.semaphore_signal(barrier, inc=1, device_id=target, device_id_type=MESH)
-    for offset in range(1, plane):
-        pl.semaphore_signal(barrier, inc=1, device_id=plane_target(offset)[1], device_id_type=MESH)
-    for offset in range(1, high):
-        pl.semaphore_signal(barrier, inc=1, device_id=line_target(offset), device_id_type=MESH)
+    reach = TOKENS + 1
+    neighbours = sum(jnp.where(route[1], 1, 0) for route in routes)
+    strangers = []
+    if low + n_fy - 2 > reach:
+        for offset in range(1, plane):
+            target = plane_target(offset)[1]
+            strangers.append((jnp.abs(target[0] - i) + jnp.abs(target[1] - j) > reach, target))
+    if (high - 1) * low > reach + 1:
+        for offset in range(1, high):
+            target = line_target(offset)
+            strangers.append((jnp.abs(target[0] - i) > reach + 1, target))
+    for strange, target in strangers:
+        @pl.when(strange)
+        def _(target=target):
+            pl.semaphore_signal(barrier, inc=1, device_id=target, device_id_type=MESH)
+
+    def pass_token(place):
+        for _, has_target, target, _ in routes:
+            @pl.when(has_target)
+            def _(target=target):
+                pl.semaphore_signal(token_sem.at[place], inc=1, device_id=target, device_id_type=MESH)
+
+    def take_token(place):
+        pl.semaphore_wait(token_sem.at[place], neighbours)
+
+    for batch in loads:
+        for load in batch:
+            load.start()
 
     g8 = lane_group(8)
     g64 = lane_group(DOF)
     g32 = lane_group(HALF)
 
     with scope("relay"):
+        pltpu.make_async_copy(right_ref, right_ref, small_sem.at[2]).wait()
+        sub = lax.broadcasted_iota(jnp.int32, (8, LANES), 0)
+        turn = (g8 - sub) % GROUPS
+        for face in range(faces):
+            for tile in range(0, DOF // GROUPS, 2):
+                x = right_ref[face // 8, face % 8, tile:tile + 2, :]
+                x = jnp.where(sub < GROUPS, jnp.broadcast_to(x[0:1], (8, LANES)), jnp.broadcast_to(x[1:2], (8, LANES)))
+                w0[face, tile * GROUPS:tile * GROUPS + 8, :] = pick(turn, rolls(x))
         small[0].wait()
-        for block in range(faces // 8):
-            for tile in range(DOF // GROUPS):
-                x = right_ref[8 * block:8 * block + 8, tile * LANES:(tile + 1) * LANES]
-                moved = rolls(x)
-                for q in range(GROUPS):
-                    wide[pl.ds(8 * block * DOF + tile * GROUPS + q, 8, stride=DOF), :] = replicate(g8, moved, q)
-        for face in range(faces):
-            w0[face] = wide[face * DOF:(face + 1) * DOF, :]
-        small[1].wait()
 
     def field_copies(power):
         return [
@@ -188,19 +226,11 @@
             picked = [field[ghost_ref[row, g]] for g in range(GROUPS)]
             send_buf[power, q] = pick(g64, picked)
         if power == 0:
-            count = sum(jnp.where(route[1], 1, 0) for route in routes) + (plane - 1) + (high - 1)
-            pl.semaphore_wait(barrier, count)
-        far_down = my_low == 0
-        starts = [
-            (1, jnp.logical_and(routes[1][1], far_down)),
-            (0, routes[0][1]),
-            (1, jnp.logical_and(routes[1][1], jnp.logical_not(far_down))),
-            (2, routes[2][1]),
-            (3, routes[3][1]),
-        ]
-        for q, needed in starts:
-            @pl.when(needed)
-            def _(copy=copies[q]):
+            pl.semaphore_wait(barrier, neighbours + sum(jnp.where(strange, 1, 0) for strange, _ in strangers))
+            pass_token(0)
+        for copy, route in zip(copies, routes):
+            @pl.when(route[1])
+            def _(copy=copy):
                 copy.start()
         return copies
 
@@ -216,7 +246,7 @@
 
     def own_products():
         for face in range(faces):
-            left = jnp.concatenate([mats[face * BLOCKS + k] for k in range(OWNED)], axis=1)
+            left = mats[face, :, :OWNED * LANES]
             right = jnp.concatenate([tiles[columns_ref[face, k]] for k in range(OWNED)], axis=0)
             out = jnp.dot(left, right, preferred_element_type=f32)
             acc[face] = out[:HALF] + out[HALF:]
@@ -224,7 +254,7 @@
     def far_products(power):
         field = fields[power + 1]
         for face in range(faces):
-            left = jnp.concatenate([mats[face * BLOCKS + k] for k in range(OWNED, BLOCKS)], axis=1)
+            left = mats[face, :, OWNED * LANES:]
             right = jnp.concatenate([tiles[columns_ref[face, k]] for k in range(OWNED, BLOCKS)], axis=0)
             out = jnp.dot(left, right, preferred_element_type=f32)
             total = acc[face] + (out[:HALF] + out[HALF:])
@@ -258,18 +288,14 @@
                 copy.wait_send()
 
     def prepare():
-        for k in range(BLOCKS):
-            for place, (first, _) in enumerate(batches):
-                if first == k:
-                    loads[place].wait()
-            for block in range(faces // 8):
-                for t in range(HALF):
-                    spread[k % 2, pl.ds(8 * block * HALF + t, 8, stride=HALF), :] = stage[
-                        k, 8 * block:8 * block + 8, t * LANES:(t + 1) * LANES]
-            for face in range(faces):
-                hi, lo = split(spread[k % 2, face * HALF:(face + 1) * HALF, :])
-                mats[face * BLOCKS + k, 0:HALF] = hi.astype(bf16)
-                mats[face * BLOCKS + k, HALF:DOF] = lo.astype(bf16)
+        for place, (first, last) in enumerate(batches):
+            whole = stage.at[first:last]
+            pltpu.make_async_copy(whole, whole, load_sem.at[place]).wait()
+            for k in range(first, last):
+                for face in range(faces):
+                    hi, lo = split(stage[k, face // 8, face % 8])
+                    mats[face, 0:HALF, k * LANES:(k + 1) * LANES] = hi.astype(bf16)
+                    mats[face, HALF:DOF, k * LANES:(k + 1) * LANES] = lo.astype(bf16)
 
     def wait_for(buf, count, sem):
         whole = buf.at[0:count]
@@ -296,19 +322,21 @@
                 src_ref=line.at[my_high], dst_ref=line.at[my_high], send_sem=gram_sem.at[which, 2],
                 recv_sem=gram_sem.at[which, 3], device_id=line_target(offset), device_id_type=MESH).start()
 
+    def add_all(buf, count):
+        terms = [buf[place] for place in range(count)]
+        while len(terms) > 1:
+            terms = [sum(terms[k:k + 2][1:], terms[k]) for k in range(0, len(terms), 2)]
+        return terms[0]
+
     def exchange_sum(which, line):
         wait_for(line, high - 1, gram_sem.at[which, 3])
-        total = line[0]
-        for place in range(1, high):
-            total = total + line[place]
-        return total
-
-    def gather(which, final, total):
-        final[my_rank] = total
+        return add_all(line, high)
+
+    def gather(which, final, first):
         for offset in range(1, plane):
             pltpu.make_async_remote_copy(
-                src_ref=final.at[my_rank], dst_ref=final.at[my_rank], send_sem=gram_sem.at[which, 4],
-                recv_sem=gram_sem.at[which, 5], device_id=plane_target(offset)[1], device_id_type=MESH).start()
+                src_ref=final.at[my_rank], dst_ref=final.at[my_rank], send_sem=gram_sem.at[which, first],
+                recv_sem=gram_sem.at[which, first + 1], device_id=plane_target(offset)[1], device_id_type=MESH).start()
 
     def gathered(which, final):
         wait_for(final, plane - 1, gram_sem.at[which, 5])
@@ -342,9 +370,7 @@
 
         both = lax.dot_general(newest[...], zbuf[...], (((0,), (0,)), ((), ())), preferred_element_type=f32)
         gram = (both[:NRHS, :LANES] + both[NRHS:2 * NRHS, LANES:]) + (both[:NRHS, LANES:] + both[NRHS:2 * NRHS, :LANES])
-        share = late_buf.shape[1]
-        for rank in range(plane):
-            late_buf[rank] = gram[rank * share:(rank + 1) * share]
+        late_plane[my_rank] = gram
 
     flat = [field.reshape(faces * DOF, LANES) for field in fields]
 
@@ -364,35 +390,42 @@
     for power in range(POWERS):
         with scope("send%d" % power):
             copies = send_field(power)
+        if power == POWERS - 1:
+            with scope("egram"):
+                early_gram()
+                scatter(0, early_buf, early_plane)
         with scope("build%d" % power):
             build_own(power)
         if power == 0:
             with scope("prepare"):
                 prepare()
-                small[2].wait()
-        if power == POWERS - 1:
-            with scope("egram"):
-                early_gram()
-                scatter(0, early_buf, early_plane)
+                small[1].wait()
         with scope("own%d" % power):
             own_products()
+        if power < TOKENS // 2:
+            take_token(2 * power)
+            pass_token(2 * power + 1)
         receive_field(power, copies)
         with scope("far%d" % power):
             far_products(power)
-
+        if power < TOKENS // 2:
+            take_token(2 * power + 1)
+            if 2 * power + 2 < TOKENS:
+                pass_token(2 * power + 2)
+
+    with scope("eplane"):
+        exchange(0, early_line, scatter_sum(0, early_buf, early_plane))
     with scope("lgram"):
         late_gram()
-        scatter(1, late_buf, late_plane)
-    with scope("eplane"):
-        exchange(0, early_line, scatter_sum(0, early_buf, early_plane))
+        gather(1, late_plane, 0)
     with scope("order"):
         order_rows()
     with scope("lplane"):
-        exchange(1, late_line, scatter_sum(1, late_buf, late_plane))
+        wait_for(late_plane, plane - 1, gram_sem.at[1, 1])
+        exchange(1, late_line, add_all(late_plane, plane))
     with scope("eline"):
-        gather(0, early_all, exchange_sum(0, early_line))
-    with scope("lline"):
-        gather(1, late_all, exchange_sum(1, late_line))
+        early_all[my_rank] = exchange_sum(0, early_line)
+        gather(0, early_all, 4)
     with scope("eall"):
         system = gathered(0, early_all)
     with scope("esolve"):
@@ -400,18 +433,19 @@
         solved = eliminate([system[t:t + 8] for t in range(0, count, 8)], True)
         spread_early = replicate(lane_group(count), rolls(solved), GROUPS - 1)
     with scope("lall"):
-        last = gathered(1, late_all)
+        last = exchange_sum(1, late_line)
     with scope("lsolve"):
         left_half = lax.broadcasted_iota(jnp.int32, (NRHS, LANES), 1) < count
         cross = jnp.where(left_half, last, 0.0)
         pad = jnp.zeros((LANES - count, LANES), f32)
         done = high_dot(cross, jnp.concatenate([solved, pad], axis=0), ((1,), (0,)))
         inner = jnp.where(left_half, done, 0.0)
+        outer = high_dot(jnp.where(lax.broadcasted_iota(jnp.int32, (count, LANES), 1) < count, solved, 0.0), jnp.concatenate([cross, jnp.zeros((LANES - NRHS, LANES), f32)], axis=0), ((1,), (1,)))
         schur = high_dot(inner, jnp.concatenate([cross, jnp.zeros((LANES - NRHS, LANES), f32)], axis=0), ((1,), (1,)))
         small_system = pltpu.roll(jnp.where(left_half, 0.0, last - done), LANES // 2, 1) - schur
         newest_part = eliminate([small_system[t:t + 8] for t in range(0, NRHS, 8)], False)
         newest_part = replicate(g32, rolls(newest_part), 1)
-        older = spread_early - high_dot(inner, newest_part, ((0,), (0,)))[:count]
+        older = spread_early - high_dot(outer[:, :NRHS], newest_part, ((1,), (0,)))
         coeffs = jnp.concatenate([older, newest_part], axis=0)
     with scope("coeffs"):
         none = jnp.zeros((NRHS, LANES), f32)
@@ -436,43 +470,54 @@
                     out_ref[8 * block:8 * block + 8, tile * LANES:(tile + 1) * LANES] = out[
                         row:row + 8, part * LANES:(part + 1) * LANES]
     with scope("drain"):
-        for which, bufs in enumerate([(early_plane, early_line, early_all), (late_plane, late_line, late_all)]):
+        for which, bufs in enumerate([(early_plane, early_line, early_all), (late_plane, late_line)]):
             for phase, (buf, amount) in enumerate(zip(bufs, (plane - 1, high - 1, plane - 1))):
                 wait_for(buf, amount, gram_sem.at[which, 2 * phase])
+
+
+def put_out(sol_ref, res_ref, sol_out, res_out, sem):
+    copies = [
+        pltpu.make_async_copy(sol_ref, sol_out, sem.at[0]),
+        pltpu.make_async_copy(res_ref, res_out, sem.at[1]),
+    ]
+    for copy in copies:
+        copy.start()
+    for copy in copies:
+        copy.wait()
 
 
 def on_device(shape, right_side, coupling, face_columns, ghost_lists):
     n_fx, n_fy, low, faces = shape
     plane = low * n_fy
     high = n_fx // low
+    right_rows = right_side.reshape(faces // 8, 8, DOF // GROUPS, LANES).transpose(0, 2, 1, 3)
+    coupling = coupling.reshape(faces // 8, 8, BLOCKS, HALF, LANES).transpose(2, 0, 3, 1, 4)
     rows = faces * DOF
     early = 2 * NRHS // plane
-    late = NRHS // plane
     vmem = pl.BlockSpec(memory_space=pltpu.VMEM)
     hbm = pl.BlockSpec(memory_space=pltpu.HBM)
     dma = pltpu.SemaphoreType.DMA
     i32 = jnp.int32
     out = jax.ShapeDtypeStruct(right_side.shape, f32)
-    gram = []
-    for share in (early, late):
-        gram += [
-            pltpu.VMEM((plane, share, LANES), f32),
-            pltpu.VMEM((plane - 1, share, LANES), f32),
-            pltpu.VMEM((high, share, LANES), f32),
-            pltpu.VMEM((plane, share, LANES), f32),
-        ]
-    return pl.pallas_call(
+    gram = [
+        pltpu.VMEM((plane, early, LANES), f32),
+        pltpu.VMEM((plane - 1, early, LANES), f32),
+        pltpu.VMEM((high, early, LANES), f32),
+        pltpu.VMEM((plane, early, LANES), f32),
+        pltpu.VMEM((plane, NRHS, LANES), f32),
+        pltpu.VMEM((high, NRHS, LANES), f32),
+    ]
+    results = pl.pallas_call(
         functools.partial(kernel, shape),
         out_shape=(out, out),
         in_specs=[hbm] * 4,
         out_specs=(vmem, vmem),
         scratch_shapes=[
-            pltpu.VMEM(right_side.shape, f32),
+            pltpu.VMEM((faces // 8, 8, DOF // GROUPS, LANES), f32),
             pltpu.SMEM(face_columns.shape, i32),
             pltpu.SMEM(ghost_lists.shape, i32),
-            pltpu.VMEM(coupling.shape, f32),
-            pltpu.VMEM((2, faces * HALF, LANES), f32),
-            pltpu.VMEM((faces * BLOCKS, DOF, LANES), bf16),
+            pltpu.VMEM((BLOCKS, faces // 8, 8, HALF, LANES), f32),
+            pltpu.VMEM((faces, DOF, BLOCKS * LANES), bf16),
         ]
         + [pltpu.VMEM((faces, DOF, LANES), f32)] * (POWERS + 1)
         + [
@@ -486,17 +531,25 @@
         ]
         + gram
         + [
-            pltpu.VMEM((rows, LANES), f32),
             dma((3,)),
             dma((-(-BLOCKS // BATCH),)),
             dma((4,)),
             dma((2, 4)),
             dma((2, 6)),
+            pltpu.SemaphoreType.REGULAR((TOKENS,)),
         ],
         compiler_params=pltpu.CompilerParams(
             collective_id=0, has_side_effects=True, vmem_limit_bytes=40 * 2**20
         ),
-    )(*[pltpu.with_memory_space_constraint(x, pltpu.HBM) for x in (right_side, coupling, face_columns, ghost_lists)])
+    )(*[pltpu.with_memory_space_constraint(x, pltpu.HBM) for x in (right_rows, coupling, face_columns, ghost_lists)])
+    return pl.pallas_call(
+        put_out,
+        out_shape=(out, out),
+        in_specs=[vmem, vmem],
+        out_specs=(hbm, hbm),
+        scratch_shapes=[dma((2,))],
+        compiler_params=pltpu.CompilerParams(vmem_limit_bytes=2**20),
+    )(*results)
 
 
 def solution(mesh):
@@ -507,7 +560,7 @@
 
     def body(right_side, coupling, face_columns, ghost_lists):
         shape = (n_fx, n_fy, low, right_side.shape[0])
-        return on_device(shape, right_side, coupling.transpose(1, 0, 2), face_columns, ghost_lists)
+        return on_device(shape, right_side, coupling, face_columns, ghost_lists)
 
     placed = (
         P(("fx", "fy"), None),

time: 33.3 us -> 29.9 us (0.90)
  Pallas kernels: 31.2 us -> 29.1 us
  local copies, waits for them, and re-layouts: 1.31 us -> 0 us
    pallas_call x1, Pallas kernels: 31.2 us -> 28.4 us  [on_device(): pl.pallas_call(functools.partial(kernel, shape), out_shape=(out, out), in...]
    unnamed x2 -> x0, local copies, waits for them, and re-layouts: 1.31 us -> none
    pallas_call x0 -> x1, Pallas kernels: none -> 0.72 us  [on_device(): pl.pallas_call(put_out, out_shape=(out, out), in_specs=[vmem, vmem], out_...]
where the time goes in v3:
time: 29.9 us; the launch traced here: 29.7 us
  Pallas kernels  29.1 us (97%)
  between operations  0.64 us (2%)
    pallas_call x1, Pallas kernels, on_device(): pl.pallas_call(functools.partial(kernel, shape), out_shape=(out, out), in...  28.4 us
    pallas_call x1, Pallas kernels, on_device(): pl.pallas_call(put_out, out_shape=(out, out), in_specs=[vmem, vmem], out_...  0.72 us

profile of v3, /device:TPU:0, one launch (start us, length us, event | category | flops | bytes accessed | tf_op | source)
XLA Modules:
  0.0 29.7 jit_solution(6236765795829837915)
XLA Ops:
  0.6 28.4 %shard_map.59 = (f32[16,2048]{1,0:T(8,128)S(1)}, f32[16,2048]{1,0:T(8,128)S(1)}) custom-call(f32[2,16,8,128]{3,2,1,0:T(8,128)} %bitcast.7, f32[11,2,32,8,128]{4,3,2,1,0:T(8,128)} %bitcast.6, s32[16,11]{1,0:T(8,128)} %columns_hbm.1, s32[4,4]{1,0:T(4,128)} %ghost_hbm.1), custom_call_target="tpu_custom_call" | custom-call | tf_op jit(solution)/shard_map/pallas_call | solution.py:510
  29.0 0.7 %shard_map.60 = (f32[16,2048]{1,0:T(8,128)}, f32[16,2048]{1,0:T(8,128)}) custom-call(f32[16,2048]{1,0:T(8,128)S(1)} %get-tuple-element.4.sol_ref, f32[16,2048]{1,0:T(8,128)S(1)} %get-tuple-element.5.res_ref), custom_call_target="tpu_custom_call" | custom-call | tf_op jit(solution)/shard_map/pallas_call | solution.py:545

commit v4 on v3

--- a/solution.py
+++ b/solution.py
@@ -15,7 +15,8 @@
 POWERS = 3
 LANES = 128
 HALF = DOF // 2
-BATCH = 3
+BATCH = 11
+PIECES = 1
 TOKENS = 2 * (POWERS - 1)
 GROUPS = LANES // NRHS
 MESH = pl.DeviceIdType.MESH
@@ -49,52 +50,50 @@
 
 def product_tile(x, group):
     hi, lo = split(x)
+    return halves(jnp.where(group < GROUPS // 2, hi, lo), group)
+
+
+def halves(x, group):
     zero = jnp.zeros_like(x)
-    top = pick(group, [hi, zero, lo, zero])
-    bottom = pick(group, [zero, hi, zero, lo])
-    return top.astype(bf16), bottom.astype(bf16)
+    even = group % 2 == 0
+    return jnp.where(even, x, zero).astype(bf16), jnp.where(even, zero, x).astype(bf16)
 
 
 def scope(name):
     return contextlib.nullcontext()
 
 
-def eliminate(tiles, inverse):
+def across_gather(x, lane):
+    return jnp.take_along_axis(x, jnp.full((8, LANES), lane, jnp.int32), axis=1)
+
+
+def across_sum(x, lane):
+    lanes = lax.broadcasted_iota(jnp.int32, (8, LANES), 1)
+    return jnp.broadcast_to(jnp.sum(jnp.where(lanes == lane, x, 0.0), axis=1, keepdims=True), (8, LANES))
+
+
+def eliminate(tiles, inverse, across):
+    tiles = list(tiles)
     sub = lax.broadcasted_iota(jnp.int32, (8, LANES), 0)
     lanes = lax.broadcasted_iota(jnp.int32, (8, LANES), 1)
 
-    def across(x, lane):
-        return jnp.broadcast_to(x[:, lane:lane + 1], (8, LANES))
-
     def down(x, row):
         return jnp.broadcast_to(x[row:row + 1, :], (8, LANES))
-
-    scales = []
-    for home, tile in enumerate(tiles):
-        diagonal = jnp.sum(jnp.where(lanes == 8 * home + sub, tile, 0.0), axis=1, keepdims=True)
-        scales.append(1.0 / jnp.broadcast_to(diagonal, (8, LANES)))
-    tiles = [tile * scale for tile, scale in zip(tiles, scales)]
 
     for home in range(len(tiles)):
         mine = tiles[home]
         cols = [across(mine, 8 * home + c) for c in range(8)]
-        for p in range(0, 8, 2):
-            q = p + 1
-            left, right = cols[p], cols[q]
-            a, b, c, d = down(left, p), down(right, p), down(left, q), down(right, q)
-            pivot = 1.0 / (a * d - b * c)
-
-            def update(x):
-                top, bottom = down(x, p), down(x, q)
-                top, bottom = d * top - b * bottom, a * bottom - c * top
-                rest = x - pivot * (left * top + right * bottom)
-                return jnp.where(sub == p, pivot * top, jnp.where(sub == q, pivot * bottom, rest))
-
+        for step in range(8):
+            pivot = 1.0 / down(cols[step], step)
+            here = sub == step
+            factor = cols[step]
             if inverse:
-                own = jnp.where(lanes == 8 * home + sub, scales[home], 0.0)
-                mine = jnp.where((lanes == 8 * home + p) | (lanes == 8 * home + q), jnp.where((sub == p) | (sub == q), own, 0.0), mine)
-            mine = update(mine)
-            cols = [update(x) if place > q else x for place, x in enumerate(cols)]
+                mine = jnp.where(lanes == 8 * home + step, jnp.where(here, 1.0, 0.0), mine)
+            scaled = down(mine, step) * pivot
+            mine = jnp.where(here, scaled, mine - factor * scaled)
+            for c in range(step + 1, 8):
+                scaled = down(cols[c], step) * pivot
+                cols[c] = jnp.where(here, scaled, cols[c] - factor * scaled)
         tiles[home] = mine
         rows8 = [down(mine, c) for c in range(8)]
         for t in [t % len(tiles) for t in range(home + 1, home + len(tiles))]:
@@ -106,13 +105,30 @@
     return jnp.concatenate(tiles, axis=0)
 
 
+def split3(x):
+    hi, rest = split(x)
+    mid, low = split(rest)
+    return [part.astype(bf16) for part in (hi, mid, low)]
+
+
 def high_dot(left, right, dims):
-    return lax.dot_general(left, right, (dims, ((), ())), precision=lax.Precision.HIGHEST, preferred_element_type=f32)
+    rows = left.shape[0]
+    along = 1 - dims[1][0]
+    left = jnp.concatenate(split3(left), axis=0)
+    right = jnp.concatenate(split3(right), axis=along)
+    out = lax.dot_general(left, right, (dims, ((), ())), preferred_element_type=f32)
+    width = out.shape[1] // 3
+
+    def block(i, j):
+        return out[i * rows:(i + 1) * rows, j * width:(j + 1) * width]
+
+    small = (block(1, 1) + block(0, 2)) + block(2, 0)
+    return block(0, 0) + ((block(0, 1) + block(1, 0)) + small)
 
 
 def kernel(shape, right_hbm, coupling_hbm, columns_hbm, ghost_hbm, sol_ref, res_ref,
            right_ref, columns_ref, ghost_ref,
-           stage, mats, w0, w1, w2, w3, tiles, acc, send_buf, recv_buf,
+           stage, mats, w0, w1, w2, w3, ordered, tiles, acc, send_buf, recv_buf,
            zbuf, newest, vbuf, early_buf, early_plane, early_line, early_all,
            late_plane, late_line,
            small_sem, load_sem, send_sem, recv_sem, gram_sem, token_sem):
@@ -185,10 +201,10 @@
         for _, has_target, target, _ in routes:
             @pl.when(has_target)
             def _(target=target):
-                pl.semaphore_signal(token_sem.at[place], inc=1, device_id=target, device_id_type=MESH)
+                pl.semaphore_signal(token_sem.at[place % 2], inc=1, device_id=target, device_id_type=MESH)
 
     def take_token(place):
-        pl.semaphore_wait(token_sem.at[place], neighbours)
+        pl.semaphore_wait(token_sem.at[place % 2], neighbours)
 
     for batch in loads:
         for load in batch:
@@ -251,9 +267,9 @@
             out = jnp.dot(left, right, preferred_element_type=f32)
             acc[face] = out[:HALF] + out[HALF:]
 
-    def far_products(power):
+    def far_products(power, part):
         field = fields[power + 1]
-        for face in range(faces):
+        for face in part:
             left = mats[face, :, OWNED * LANES:]
             right = jnp.concatenate([tiles[columns_ref[face, k]] for k in range(OWNED, BLOCKS)], axis=0)
             out = jnp.dot(left, right, preferred_element_type=f32)
@@ -261,8 +277,32 @@
             total = total + pltpu.roll(total, LANES // 2, 1)
             turned = pltpu.roll(total, NRHS, 1)
             even = g32 % 2 == 0
-            field[face, pl.ds(0, HALF, stride=2), :] = jnp.where(even, total, turned)
-            field[face, pl.ds(1, HALF, stride=2), :] = jnp.where(even, turned, total)
+            first, second = jnp.where(even, total, turned), jnp.where(even, turned, total)
+            field[face, pl.ds(0, HALF, stride=2), :] = first
+            field[face, pl.ds(1, HALF, stride=2), :] = second
+            both = jnp.concatenate([first, second], axis=0)
+            if power < POWERS - 1:
+                ordered[power + 1, face] = both
+            else:
+                late_rows(face, both)
+
+    def first_rows():
+        for face in range(faces):
+            rows = slice(face * DOF, (face + 1) * DOF)
+            a = jnp.concatenate([w0[face, pl.ds(parity, HALF, stride=2), :] for parity in range(2)], axis=0)
+            hi, lo = split(pick(g64, [a + ordered[1, face], jnp.zeros_like(a), jnp.zeros_like(a), a]))
+            zbuf[rows, :LANES] = hi.astype(bf16)
+            zbuf[rows, LANES:] = lo.astype(bf16)
+            newest[rows, :] = jnp.where(g64 < 2, hi, pltpu.roll(lo, LANES // 2, 1)).astype(bf16)
+
+    def late_rows(face, newer):
+        rows = slice(face * DOF, (face + 1) * DOF)
+        hi, lo = split(ordered[POWERS - 1, face] + newer)
+        zero = jnp.zeros_like(hi)
+        third = g64 == POWERS - 1
+        zbuf[rows, :LANES] = zbuf[rows, :LANES] + jnp.where(third, hi, zero).astype(bf16)
+        zbuf[rows, LANES:] = zbuf[rows, LANES:] + jnp.where(third, lo, zero).astype(bf16)
+        newest[rows, :] = jnp.where(g64 == 0, hi, lo).astype(bf16)
 
     def receive_field(power, copies):
         for q in (2, 3, 0, 1):
@@ -277,9 +317,12 @@
                 def _(q=q):
                     recv_buf[power, q] = jnp.zeros((DOF, LANES), f32)
             with scope("conv%d_%d" % (power, q)):
-                moved = rolls(recv_buf[power, q])
+                hi, lo = split(recv_buf[power, q])
+                hi, lo = rolls(hi), rolls(lo)
                 for g in range(GROUPS):
-                    top, bottom = product_tile(replicate(g64, moved, g), g64)
+                    top, bottom = halves(pick(g64, [
+                        (hi if lane < GROUPS // 2 else lo)[(lane - g) % GROUPS] for lane in range(GROUPS)
+                    ]), g64)
                     tiles[faces + q * GROUPS + g, 0:DOF] = top
                     tiles[faces + q * GROUPS + g, DOF:2 * DOF] = bottom
 
@@ -346,29 +389,22 @@
         @pl.loop(0, faces, unroll=4)
         def _(face):
             rows = pl.ds(pl.multiple_of(face * DOF, DOF), DOF)
-            a, b, c = w0[face], w1[face], w2[face]
-            hi, lo = split(pick(g64, [a + b, b + c, jnp.zeros_like(a), a]))
-            zbuf[rows, :LANES] = hi.astype(bf16)
-            zbuf[rows, LANES:] = lo.astype(bf16)
-
-        z = zbuf[...]
-        both = lax.dot_general(z, z, (((0,), (0,)), ((), ())), preferred_element_type=f32)
-        gram = (both[:LANES, :LANES] + both[LANES:, LANES:]) + (both[:LANES, LANES:] + both[LANES:, :LANES])
+            hi, lo = split(ordered[1, face] + ordered[2, face])
+            hi, lo = hi.astype(bf16), lo.astype(bf16)
+            second = g64 == 1
+            zbuf[rows, :LANES] = jnp.where(second, hi, zbuf[rows, :LANES])
+            zbuf[rows, LANES:] = jnp.where(second, lo, zbuf[rows, LANES:])
+            newest[rows, :] = jnp.where(second, hi, jnp.where(g64 == 3, lo, newest[rows, :]))
+
+        both = lax.dot_general(newest[...], zbuf[...], (((0,), (0,)), ((), ())), preferred_element_type=f32)
+        half = 2 * NRHS
+        gram = (both[:half, :LANES] + both[half:, LANES:]) + (both[:half, LANES:] + both[half:, :LANES])
         share = early_buf.shape[1]
         for rank in range(plane):
             early_buf[rank] = gram[rank * share:(rank + 1) * share]
 
     def late_gram():
-        @pl.loop(0, faces, unroll=4)
-        def _(face):
-            rows = pl.ds(pl.multiple_of(face * DOF, DOF), DOF)
-            hi, lo = split(w2[face] + w3[face])
-            zero = jnp.zeros_like(hi)
-            zbuf[rows, :LANES] = zbuf[rows, :LANES] + pick(g64, [zero, zero, hi, zero]).astype(bf16)
-            zbuf[rows, LANES:] = zbuf[rows, LANES:] + pick(g64, [zero, zero, lo, zero]).astype(bf16)
-            newest[rows, :] = pick(g64, [hi, lo, zero, zero]).astype(bf16)
-
-        both = lax.dot_general(newest[...], zbuf[...], (((0,), (0,)), ((), ())), preferred_element_type=f32)
+        both = lax.dot_general(newest[:, :2 * NRHS], zbuf[...], (((0,), (0,)), ((), ())), preferred_element_type=f32)
         gram = (both[:NRHS, :LANES] + both[NRHS:2 * NRHS, LANES:]) + (both[:NRHS, LANES:] + both[NRHS:2 * NRHS, :LANES])
         late_plane[my_rank] = gram
 
@@ -402,35 +438,39 @@
                 small[1].wait()
         with scope("own%d" % power):
             own_products()
+        if power == 1:
+            first_rows()
         if power < TOKENS // 2:
             take_token(2 * power)
             pass_token(2 * power + 1)
         receive_field(power, copies)
         with scope("far%d" % power):
-            far_products(power)
+            far_products(power, range(faces // 2))
+            if power == POWERS - 1:
+                with scope("eplane"):
+                    exchange(0, early_line, scatter_sum(0, early_buf, early_plane))
+            far_products(power, range(faces // 2, faces))
         if power < TOKENS // 2:
             take_token(2 * power + 1)
             if 2 * power + 2 < TOKENS:
                 pass_token(2 * power + 2)
 
-    with scope("eplane"):
-        exchange(0, early_line, scatter_sum(0, early_buf, early_plane))
     with scope("lgram"):
         late_gram()
         gather(1, late_plane, 0)
     with scope("order"):
         order_rows()
+    with scope("eline"):
+        early_all[my_rank] = exchange_sum(0, early_line)
+        gather(0, early_all, 4)
     with scope("lplane"):
         wait_for(late_plane, plane - 1, gram_sem.at[1, 1])
         exchange(1, late_line, add_all(late_plane, plane))
-    with scope("eline"):
-        early_all[my_rank] = exchange_sum(0, early_line)
-        gather(0, early_all, 4)
     with scope("eall"):
         system = gathered(0, early_all)
     with scope("esolve"):
         count = 2 * NRHS
-        solved = eliminate([system[t:t + 8] for t in range(0, count, 8)], True)
+        solved = eliminate([system[t:t + 8] for t in range(0, count, 8)], True, across_gather)
         spread_early = replicate(lane_group(count), rolls(solved), GROUPS - 1)
     with scope("lall"):
         last = exchange_sum(1, late_line)
@@ -443,7 +483,7 @@
         outer = high_dot(jnp.where(lax.broadcasted_iota(jnp.int32, (count, LANES), 1) < count, solved, 0.0), jnp.concatenate([cross, jnp.zeros((LANES - NRHS, LANES), f32)], axis=0), ((1,), (1,)))
         schur = high_dot(inner, jnp.concatenate([cross, jnp.zeros((LANES - NRHS, LANES), f32)], axis=0), ((1,), (1,)))
         small_system = pltpu.roll(jnp.where(left_half, 0.0, last - done), LANES // 2, 1) - schur
-        newest_part = eliminate([small_system[t:t + 8] for t in range(0, NRHS, 8)], False)
+        newest_part = eliminate([small_system[t:t + 8] for t in range(0, NRHS, 8)], False, across_sum)
         newest_part = replicate(g32, rolls(newest_part), 1)
         older = spread_early - high_dot(outer[:, :NRHS], newest_part, ((1,), (0,)))
         coeffs = jnp.concatenate([older, newest_part], axis=0)
@@ -476,9 +516,10 @@
 
 
 def put_out(sol_ref, res_ref, sol_out, res_out, sem):
+    width = sol_ref.shape[1] // PIECES
     copies = [
-        pltpu.make_async_copy(sol_ref, sol_out, sem.at[0]),
-        pltpu.make_async_copy(res_ref, res_out, sem.at[1]),
+        pltpu.make_async_copy(src.at[:, pl.ds(piece * width, width)], dst.at[:, pl.ds(piece * width, width)], sem.at[part, piece])
+        for part, (src, dst) in enumerate([(sol_ref, sol_out), (res_ref, res_out)]) for piece in range(PIECES)
     ]
     for copy in copies:
         copy.start()
@@ -521,6 +562,7 @@
         ]
         + [pltpu.VMEM((faces, DOF, LANES), f32)] * (POWERS + 1)
         + [
+            pltpu.VMEM((POWERS, faces, DOF, LANES), f32),
             pltpu.VMEM((faces + 4 * GROUPS, LANES, LANES), bf16),
             pltpu.VMEM((faces, HALF, LANES), f32),
             pltpu.VMEM((POWERS, 4, DOF, LANES), f32),
@@ -536,7 +578,7 @@
             dma((4,)),
             dma((2, 4)),
             dma((2, 6)),
-            pltpu.SemaphoreType.REGULAR((TOKENS,)),
+            pltpu.SemaphoreType.REGULAR((2,)),
         ],
         compiler_params=pltpu.CompilerParams(
             collective_id=0, has_side_effects=True, vmem_limit_bytes=40 * 2**20
@@ -547,7 +589,7 @@
         out_shape=(out, out),
         in_specs=[vmem, vmem],
         out_specs=(hbm, hbm),
-        scratch_shapes=[dma((2,))],
+        scratch_shapes=[dma((2, PIECES))],
         compiler_params=pltpu.CompilerParams(vmem_limit_bytes=2**20),
     )(*results)
 

time: 29.9 us -> 29.2 us (0.977)
  Pallas kernels: 29.1 us -> 28.3 us
    pallas_call x1, Pallas kernels: 28.4 us -> 27.6 us  [on_device(): pl.pallas_call(functools.partial(kernel, shape), out_shape=(out, out), in...]
where the time goes in v4:
time: 29.2 us; the launch traced here: 28.9 us
  Pallas kernels  28.3 us (97%)
  between operations  0.64 us (2%)
    pallas_call x1, Pallas kernels, on_device(): pl.pallas_call(functools.partial(kernel, shape), out_shape=(out, out), in...  27.6 us
    pallas_call x1, Pallas kernels, on_device(): pl.pallas_call(put_out, out_shape=(out, out), in_specs=[vmem, vmem], out_...  0.72 us

profile of v4, /device:TPU:0, one launch (start us, length us, event | category | flops | bytes accessed | tf_op | source)
XLA Modules:
  0.0 28.9 jit_solution(15908488958287464638)
XLA Ops:
  0.6 27.6 %shard_map.59 = (f32[16,2048]{1,0:T(8,128)S(1)}, f32[16,2048]{1,0:T(8,128)S(1)}) custom-call(f32[2,16,8,128]{3,2,1,0:T(8,128)} %bitcast.7, f32[11,2,32,8,128]{4,3,2,1,0:T(8,128)} %bitcast.6, s32[16,11]{1,0:T(8,128)} %columns_hbm.1, s32[4,4]{1,0:T(4,128)} %ghost_hbm.1), custom_call_target="tpu_custom_call" | custom-call | tf_op jit(solution)/shard_map/pallas_call | solution.py:551
  28.2 0.7 %shard_map.60 = (f32[16,2048]{1,0:T(8,128)}, f32[16,2048]{1,0:T(8,128)}) custom-call(f32[16,2048]{1,0:T(8,128)S(1)} %get-tuple-element.4.sol_ref, f32[16,2048]{1,0:T(8,128)S(1)} %get-tuple-element.5.res_ref), custom_call_target="tpu_custom_call" | custom-call | tf_op jit(solution)/shard_map/pallas_call | solution.py:587

commit v5 on v4

--- a/solution.py
+++ b/solution.py
@@ -235,20 +235,29 @@
             for q in range(4)
         ]
 
-    def send_field(power):
+    def start_copies(copies, directions):
+        for q in directions:
+            @pl.when(routes[q][1])
+            def _(copy=copies[q]):
+                copy.start()
+
+    def send_field(power, copies, directions):
         field = fields[power]
-        copies = field_copies(power)
-        for q, (row, _, _, _) in enumerate(routes):
-            picked = [field[ghost_ref[row, g]] for g in range(GROUPS)]
+        for q in directions:
+            picked = [field[ghost_ref[routes[q][0], g]] for g in range(GROUPS)]
             send_buf[power, q] = pick(g64, picked)
         if power == 0:
             pl.semaphore_wait(barrier, neighbours + sum(jnp.where(strange, 1, 0) for strange, _ in strangers))
             pass_token(0)
-        for copy, route in zip(copies, routes):
-            @pl.when(route[1])
-            def _(copy=copy):
-                copy.start()
-        return copies
+        start_copies(copies, directions)
+
+    def send_products(power, copies, directions):
+        listed = {q: [ghost_ref[routes[q][0], g] for g in range(GROUPS)] for q in directions}
+        for q in directions:
+            pairs = [far_rows(face) for face in listed[q]]
+            for parity in range(2):
+                send_buf[power, q, pl.ds(parity, HALF, stride=2), :] = pick(g32, [pair[parity] for pair in pairs])
+        start_copies(copies, directions)
 
     def build_own(power):
         field = fields[power]
@@ -267,17 +276,20 @@
             out = jnp.dot(left, right, preferred_element_type=f32)
             acc[face] = out[:HALF] + out[HALF:]
 
+    def far_rows(face):
+        left = mats[face, :, OWNED * LANES:]
+        right = jnp.concatenate([tiles[columns_ref[face, k]] for k in range(OWNED, BLOCKS)], axis=0)
+        out = jnp.dot(left, right, preferred_element_type=f32)
+        total = acc[face] + (out[:HALF] + out[HALF:])
+        total = total + pltpu.roll(total, LANES // 2, 1)
+        turned = pltpu.roll(total, NRHS, 1)
+        even = g32 % 2 == 0
+        return jnp.where(even, total, turned), jnp.where(even, turned, total)
+
     def far_products(power, part):
         field = fields[power + 1]
         for face in part:
-            left = mats[face, :, OWNED * LANES:]
-            right = jnp.concatenate([tiles[columns_ref[face, k]] for k in range(OWNED, BLOCKS)], axis=0)
-            out = jnp.dot(left, right, preferred_element_type=f32)
-            total = acc[face] + (out[:HALF] + out[HALF:])
-            total = total + pltpu.roll(total, LANES // 2, 1)
-            turned = pltpu.roll(total, NRHS, 1)
-            even = g32 % 2 == 0
-            first, second = jnp.where(even, total, turned), jnp.where(even, turned, total)
+            first, second = far_rows(face)
             field[face, pl.ds(0, HALF, stride=2), :] = first
             field[face, pl.ds(1, HALF, stride=2), :] = second
             both = jnp.concatenate([first, second], axis=0)
@@ -423,9 +435,10 @@
                     vbuf[q, row:row + 16, :LANES] = hi.astype(bf16)
                     vbuf[q, row:row + 16, LANES:] = lo.astype(bf16)
 
+    copies = field_copies(0)
+    with scope("send0"):
+        send_field(0, copies, range(4))
     for power in range(POWERS):
-        with scope("send%d" % power):
-            copies = send_field(power)
         if power == POWERS - 1:
             with scope("egram"):
                 early_gram()
@@ -444,16 +457,24 @@
             take_token(2 * power)
             pass_token(2 * power + 1)
         receive_field(power, copies)
-        with scope("far%d" % power):
-            far_products(power, range(faces // 2))
-            if power == POWERS - 1:
-                with scope("eplane"):
-                    exchange(0, early_line, scatter_sum(0, early_buf, early_plane))
-            far_products(power, range(faces // 2, faces))
         if power < TOKENS // 2:
             take_token(2 * power + 1)
             if 2 * power + 2 < TOKENS:
                 pass_token(2 * power + 2)
+        if power < POWERS - 1:
+            copies = field_copies(power + 1)
+            with scope("send%d" % (power + 1)):
+                send_products(power + 1, copies, (0, 1))
+            with scope("far%d" % power):
+                far_products(power, range(faces))
+            with scope("sendy%d" % (power + 1)):
+                send_field(power + 1, copies, (2, 3))
+        else:
+            with scope("far%d" % power):
+                far_products(power, range(faces // 2))
+                with scope("eplane"):
+                    exchange(0, early_line, scatter_sum(0, early_buf, early_plane))
+                far_products(power, range(faces // 2, faces))
 
     with scope("lgram"):
         late_gram()

time: 29.2 us -> 29 us (level)
  no operation moved by 1% of the time
where the time goes in v5:
time: 29 us; the launch traced here: 28.8 us
  Pallas kernels  28.1 us (97%)
  between operations  0.64 us (2%)
    pallas_call x1, Pallas kernels, on_device(): pl.pallas_call(functools.partial(kernel, shape), out_shape=(out, out), in...  27.4 us
    pallas_call x1, Pallas kernels, on_device(): pl.pallas_call(put_out, out_shape=(out, out), in_specs=[vmem, vmem], out_...  0.72 us

profile of v5, /device:TPU:0, one launch (start us, length us, event | category | flops | bytes accessed | tf_op | source)
XLA Modules:
  0.0 28.8 jit_solution(15227058510915091239)
XLA Ops:
  0.6 27.4 %shard_map.59 = (f32[16,2048]{1,0:T(8,128)S(1)}, f32[16,2048]{1,0:T(8,128)S(1)}) custom-call(f32[2,16,8,128]{3,2,1,0:T(8,128)} %bitcast.7, f32[11,2,32,8,128]{4,3,2,1,0:T(8,128)} %bitcast.6, s32[16,11]{1,0:T(8,128)} %columns_hbm.1, s32[4,4]{1,0:T(4,128)} %ghost_hbm.1), custom_call_target="tpu_custom_call" | custom-call | tf_op jit(solution)/shard_map/pallas_call | solution.py:572
  28.1 0.7 %shard_map.60 = (f32[16,2048]{1,0:T(8,128)}, f32[16,2048]{1,0:T(8,128)}) custom-call(f32[16,2048]{1,0:T(8,128)S(1)} %get-tuple-element.4.sol_ref, f32[16,2048]{1,0:T(8,128)S(1)} %get-tuple-element.5.res_ref), custom_call_target="tpu_custom_call" | custom-call | tf_op jit(solution)/shard_map/pallas_call | solution.py:608

commit v6 on v5

--- a/solution.py
+++ b/solution.py
@@ -72,8 +72,8 @@
     return jnp.broadcast_to(jnp.sum(jnp.where(lanes == lane, x, 0.0), axis=1, keepdims=True), (8, LANES))
 
 
-def eliminate(tiles, inverse, across):
-    tiles = list(tiles)
+def eliminate(tiles, inverse, across, rights=()):
+    tiles, rights = list(tiles), list(rights)
     sub = lax.broadcasted_iota(jnp.int32, (8, LANES), 0)
     lanes = lax.broadcasted_iota(jnp.int32, (8, LANES), 1)
 
@@ -91,18 +91,27 @@
                 mine = jnp.where(lanes == 8 * home + step, jnp.where(here, 1.0, 0.0), mine)
             scaled = down(mine, step) * pivot
             mine = jnp.where(here, scaled, mine - factor * scaled)
+            if rights:
+                scaled = down(rights[home], step) * pivot
+                rights[home] = jnp.where(here, scaled, rights[home] - factor * scaled)
             for c in range(step + 1, 8):
                 scaled = down(cols[c], step) * pivot
                 cols[c] = jnp.where(here, scaled, cols[c] - factor * scaled)
         tiles[home] = mine
         rows8 = [down(mine, c) for c in range(8)]
         for t in [t % len(tiles) for t in range(home + 1, home + len(tiles))]:
-            terms = [across(tiles[t], 8 * home + c) * rows8[c] for c in range(8)]
-            while len(terms) > 1:
-                terms = [terms[k] + terms[k + 1] for k in range(0, len(terms), 2)]
+            factors = [across(tiles[t], 8 * home + c) for c in range(8)]
             base = jnp.where(lanes // 8 == home, 0.0, tiles[t]) if inverse else tiles[t]
-            tiles[t] = base - terms[0]
-    return jnp.concatenate(tiles, axis=0)
+            tiles[t] = base - tree([factor * row for factor, row in zip(factors, rows8)])
+            if rights:
+                rights[t] = rights[t] - tree([factor * down(rights[home], c) for c, factor in enumerate(factors)])
+    return jnp.concatenate(rights or tiles, axis=0)
+
+
+def tree(terms):
+    while len(terms) > 1:
+        terms = [terms[k] + terms[k + 1] for k in range(0, len(terms), 2)]
+    return terms[0]
 
 
 def split3(x):
@@ -156,6 +165,12 @@
         (3, j < n_fy - 1, (i, j + 1), j > 0),
         (2, j > 0, (i, j - 1), j < n_fy - 1),
     ]
+
+    barrier = pltpu.get_barrier_semaphore()
+    for _, has_target, target, _ in routes:
+        @pl.when(has_target)
+        def _(target=target):
+            pl.semaphore_signal(barrier, inc=1, device_id=target, device_id_type=MESH)
 
     small = [
         pltpu.make_async_copy(src, dst, small_sem.at[place])
@@ -176,11 +191,6 @@
         ]
         for place, (first, last) in enumerate(batches)
     ]
-    barrier = pltpu.get_barrier_semaphore()
-    for _, has_target, target, _ in routes:
-        @pl.when(has_target)
-        def _(target=target):
-            pl.semaphore_signal(barrier, inc=1, device_id=target, device_id_type=MESH)
     reach = TOKENS + 1
     neighbours = sum(jnp.where(route[1], 1, 0) for route in routes)
     strangers = []
@@ -248,8 +258,9 @@
             send_buf[power, q] = pick(g64, picked)
         if power == 0:
             pl.semaphore_wait(barrier, neighbours + sum(jnp.where(strange, 1, 0) for strange, _ in strangers))
+        start_copies(copies, directions)
+        if power == 0:
             pass_token(0)
-        start_copies(copies, directions)
 
     def send_products(power, copies, directions):
         listed = {q: [ghost_ref[routes[q][0], g] for g in range(GROUPS)] for q in directions}
@@ -316,29 +327,30 @@
         zbuf[rows, LANES:] = zbuf[rows, LANES:] + jnp.where(third, lo, zero).astype(bf16)
         newest[rows, :] = jnp.where(g64 == 0, hi, lo).astype(bf16)
 
-    def receive_field(power, copies):
-        for q in (2, 3, 0, 1):
-            _, has_target, _, has_source = routes[q]
-
-            with scope("recv%d_%d" % (power, q)):
-                @pl.when(has_source)
-                def _(copy=copies[q]):
-                    copy.wait_recv()
-
-                @pl.when(jnp.logical_not(has_source))
-                def _(q=q):
-                    recv_buf[power, q] = jnp.zeros((DOF, LANES), f32)
-            with scope("conv%d_%d" % (power, q)):
-                hi, lo = split(recv_buf[power, q])
-                hi, lo = rolls(hi), rolls(lo)
-                for g in range(GROUPS):
-                    top, bottom = halves(pick(g64, [
-                        (hi if lane < GROUPS // 2 else lo)[(lane - g) % GROUPS] for lane in range(GROUPS)
-                    ]), g64)
-                    tiles[faces + q * GROUPS + g, 0:DOF] = top
-                    tiles[faces + q * GROUPS + g, DOF:2 * DOF] = bottom
-
-            @pl.when(has_target)
+    def receive_field(power, copies, directions):
+        for q in directions:
+            has_source = routes[q][3]
+
+            @pl.when(has_source)
+            def _(copy=copies[q]):
+                copy.wait_recv()
+
+            @pl.when(jnp.logical_not(has_source))
+            def _(q=q):
+                recv_buf[power, q] = jnp.zeros((DOF, LANES), f32)
+        for q in directions:
+            hi, lo = split(recv_buf[power, q])
+            hi, lo = rolls(hi), rolls(lo)
+            for g in range(GROUPS):
+                top, bottom = halves(pick(g64, [
+                    (hi if lane < GROUPS // 2 else lo)[(lane - g) % GROUPS] for lane in range(GROUPS)
+                ]), g64)
+                tiles[faces + q * GROUPS + g, 0:DOF] = top
+                tiles[faces + q * GROUPS + g, DOF:2 * DOF] = bottom
+
+    def finish_sends(copies):
+        for q in range(4):
+            @pl.when(routes[q][1])
             def _(copy=copies[q]):
                 copy.wait_send()
 
@@ -456,15 +468,19 @@
         if power < TOKENS // 2:
             take_token(2 * power)
             pass_token(2 * power + 1)
-        receive_field(power, copies)
-        if power < TOKENS // 2:
-            take_token(2 * power + 1)
-            if 2 * power + 2 < TOKENS:
-                pass_token(2 * power + 2)
+        with scope("recvy%d" % power):
+            receive_field(power, copies, (2, 3))
+            finish_sends(copies)
+            if power < TOKENS // 2:
+                take_token(2 * power + 1)
+        with scope("recvx%d" % power):
+            receive_field(power, copies, (0, 1))
         if power < POWERS - 1:
             copies = field_copies(power + 1)
             with scope("send%d" % (power + 1)):
                 send_products(power + 1, copies, (0, 1))
+            if power < TOKENS // 2 and 2 * power + 2 < TOKENS:
+                pass_token(2 * power + 2)
             with scope("far%d" % power):
                 far_products(power, range(faces))
             with scope("sendy%d" % (power + 1)):
@@ -503,9 +519,12 @@
         inner = jnp.where(left_half, done, 0.0)
         outer = high_dot(jnp.where(lax.broadcasted_iota(jnp.int32, (count, LANES), 1) < count, solved, 0.0), jnp.concatenate([cross, jnp.zeros((LANES - NRHS, LANES), f32)], axis=0), ((1,), (1,)))
         schur = high_dot(inner, jnp.concatenate([cross, jnp.zeros((LANES - NRHS, LANES), f32)], axis=0), ((1,), (1,)))
-        small_system = pltpu.roll(jnp.where(left_half, 0.0, last - done), LANES // 2, 1) - schur
-        newest_part = eliminate([small_system[t:t + 8] for t in range(0, NRHS, 8)], False, across_sum)
-        newest_part = replicate(g32, rolls(newest_part), 1)
+        turned = rolls(last - done)
+        small_system = turned[GROUPS // 2] - schur
+        rights = replicate(g32, turned, GROUPS - 1)
+        cuts = range(0, NRHS, 8)
+        newest_part = eliminate(
+            [small_system[t:t + 8] for t in cuts], False, across_sum, [rights[t:t + 8] for t in cuts])
         older = spread_early - high_dot(outer[:, :NRHS], newest_part, ((1,), (0,)))
         coeffs = jnp.concatenate([older, newest_part], axis=0)
     with scope("coeffs"):

time: 29 us -> 28.9 us (level)
  no operation moved by 1% of the time
where the time goes in v6:
time: 28.9 us; the launch traced here: 28.6 us
  Pallas kernels  28 us (97%)
  between operations  0.64 us (2%)
    pallas_call x1, Pallas kernels, on_device(): pl.pallas_call(functools.partial(kernel, shape), out_shape=(out, out), in...  27.3 us
    pallas_call x1, Pallas kernels, on_device(): pl.pallas_call(put_out, out_shape=(out, out), in_specs=[vmem, vmem], out_...  0.72 us

profile of v6, /device:TPU:0, one launch (start us, length us, event | category | flops | bytes accessed | tf_op | source)
XLA Modules:
  0.0 28.6 jit_solution(751768102620089837)
XLA Ops:
  0.6 27.3 %shard_map.59 = (f32[16,2048]{1,0:T(8,128)S(1)}, f32[16,2048]{1,0:T(8,128)S(1)}) custom-call(f32[2,16,8,128]{3,2,1,0:T(8,128)} %bitcast.7, f32[11,2,32,8,128]{4,3,2,1,0:T(8,128)} %bitcast.6, s32[16,11]{1,0:T(8,128)} %columns_hbm.1, s32[4,4]{1,0:T(4,128)} %ghost_hbm.1), custom_call_target="tpu_custom_call" | custom-call | tf_op jit(solution)/shard_map/pallas_call | solution.py:591
  27.9 0.7 %shard_map.60 = (f32[16,2048]{1,0:T(8,128)}, f32[16,2048]{1,0:T(8,128)}) custom-call(f32[16,2048]{1,0:T(8,128)S(1)} %get-tuple-element.4.sol_ref, f32[16,2048]{1,0:T(8,128)S(1)} %get-tuple-element.5.res_ref), custom_call_target="tpu_custom_call" | custom-call | tf_op jit(solution)/shard_map/pallas_call | solution.py:627

commit v7 on v6

--- a/solution.py
+++ b/solution.py
@@ -372,12 +372,12 @@
         for offset in range(1, plane):
             rank, target = plane_target(offset)
             pltpu.make_async_remote_copy(
-                src_ref=buf.at[rank], dst_ref=landed.at[offset - 1], send_sem=gram_sem.at[which, 0],
-                recv_sem=gram_sem.at[which, 1], device_id=target, device_id_type=MESH).start()
+                src_ref=buf.at[rank], dst_ref=landed.at[offset - 1], send_sem=gram_sem.at[4 * which],
+                recv_sem=gram_sem.at[4 * which + 1], device_id=target, device_id_type=MESH).start()
 
     def scatter_sum(which, buf, landed):
         total = buf[my_rank]
-        wait_for(landed, plane - 1, gram_sem.at[which, 1])
+        wait_for(landed, plane - 1, gram_sem.at[4 * which + 1])
         for offset in range(1, plane):
             total = total + landed[offset - 1]
         return total
@@ -386,8 +386,8 @@
         line[my_high] = total
         for offset in range(1, high):
             pltpu.make_async_remote_copy(
-                src_ref=line.at[my_high], dst_ref=line.at[my_high], send_sem=gram_sem.at[which, 2],
-                recv_sem=gram_sem.at[which, 3], device_id=line_target(offset), device_id_type=MESH).start()
+                src_ref=line.at[my_high], dst_ref=line.at[my_high], send_sem=gram_sem.at[4 * which],
+                recv_sem=gram_sem.at[4 * which + 2], device_id=line_target(offset), device_id_type=MESH).start()
 
     def add_all(buf, count):
         terms = [buf[place] for place in range(count)]
@@ -396,17 +396,17 @@
         return terms[0]
 
     def exchange_sum(which, line):
-        wait_for(line, high - 1, gram_sem.at[which, 3])
+        wait_for(line, high - 1, gram_sem.at[4 * which + 2])
         return add_all(line, high)
 
     def gather(which, final, first):
         for offset in range(1, plane):
             pltpu.make_async_remote_copy(
-                src_ref=final.at[my_rank], dst_ref=final.at[my_rank], send_sem=gram_sem.at[which, first],
-                recv_sem=gram_sem.at[which, first + 1], device_id=plane_target(offset)[1], device_id_type=MESH).start()
+                src_ref=final.at[my_rank], dst_ref=final.at[my_rank], send_sem=gram_sem.at[4 * which],
+                recv_sem=gram_sem.at[4 * which + first], device_id=plane_target(offset)[1], device_id_type=MESH).start()
 
     def gathered(which, final):
-        wait_for(final, plane - 1, gram_sem.at[which, 5])
+        wait_for(final, plane - 1, gram_sem.at[4 * which + 3])
         return jnp.concatenate([final[rank] for rank in range(plane)], axis=0)
 
     def early_gram():
@@ -494,14 +494,14 @@
 
     with scope("lgram"):
         late_gram()
-        gather(1, late_plane, 0)
+        gather(1, late_plane, 1)
     with scope("order"):
         order_rows()
     with scope("eline"):
         early_all[my_rank] = exchange_sum(0, early_line)
-        gather(0, early_all, 4)
+        gather(0, early_all, 3)
     with scope("lplane"):
-        wait_for(late_plane, plane - 1, gram_sem.at[1, 1])
+        wait_for(late_plane, plane - 1, gram_sem.at[5])
         exchange(1, late_line, add_all(late_plane, plane))
     with scope("eall"):
         system = gathered(0, early_all)
@@ -550,9 +550,10 @@
                     out_ref[8 * block:8 * block + 8, tile * LANES:(tile + 1) * LANES] = out[
                         row:row + 8, part * LANES:(part + 1) * LANES]
     with scope("drain"):
-        for which, bufs in enumerate([(early_plane, early_line, early_all), (late_plane, late_line)]):
-            for phase, (buf, amount) in enumerate(zip(bufs, (plane - 1, high - 1, plane - 1))):
-                wait_for(buf, amount, gram_sem.at[which, 2 * phase])
+        sized = ordered.reshape(POWERS * faces * DOF, LANES)
+        sent = 2 * (plane - 1) + high - 1
+        wait_for(sized, sent * early_buf.shape[1], gram_sem.at[0])
+        wait_for(sized, (sent - plane + 1) * NRHS, gram_sem.at[4])
 
 
 def put_out(sol_ref, res_ref, sol_out, res_out, sem):
@@ -617,7 +618,7 @@
             dma((-(-BLOCKS // BATCH),)),
             dma((4,)),
             dma((2, 4)),
-            dma((2, 6)),
+            dma((7,)),
             pltpu.SemaphoreType.REGULAR((2,)),
         ],
         compiler_params=pltpu.CompilerParams(

time: 28.9 us -> 28.8 us (level)
  no operation moved by 1% of the time
where the time goes in v7:
time: 28.8 us; the launch traced here: 28.6 us
  Pallas kernels  27.9 us (97%)
  between operations  0.64 us (2%)
    pallas_call x1, Pallas kernels, on_device(): pl.pallas_call(functools.partial(kernel, shape), out_shape=(out, out), in...  27.2 us
    pallas_call x1, Pallas kernels, on_device(): pl.pallas_call(put_out, out_shape=(out, out), in_specs=[vmem, vmem], out_...  0.72 us

profile of v7, /device:TPU:0, one launch (start us, length us, event | category | flops | bytes accessed | tf_op | source)
XLA Modules:
  0.0 28.6 jit_solution(2933333326801928393)
XLA Ops:
  0.6 27.2 %shard_map.59 = (f32[16,2048]{1,0:T(8,128)S(1)}, f32[16,2048]{1,0:T(8,128)S(1)}) custom-call(f32[2,16,8,128]{3,2,1,0:T(8,128)} %bitcast.7, f32[11,2,32,8,128]{4,3,2,1,0:T(8,128)} %bitcast.6, s32[16,11]{1,0:T(8,128)} %columns_hbm.1, s32[4,4]{1,0:T(4,128)} %ghost_hbm.1), custom_call_target="tpu_custom_call" | custom-call | tf_op jit(solution)/shard_map/pallas_call | solution.py:592
  27.9 0.7 %shard_map.60 = (f32[16,2048]{1,0:T(8,128)}, f32[16,2048]{1,0:T(8,128)}) custom-call(f32[16,2048]{1,0:T(8,128)S(1)} %get-tuple-element.4.sol_ref, f32[16,2048]{1,0:T(8,128)S(1)} %get-tuple-element.5.res_ref), custom_call_target="tpu_custom_call" | custom-call | tf_op jit(solution)/shard_map/pallas_call | solution.py:628

commit v8 on v7

--- a/solution.py
+++ b/solution.py
@@ -306,6 +306,8 @@
             both = jnp.concatenate([first, second], axis=0)
             if power < POWERS - 1:
                 ordered[power + 1, face] = both
+                if power == POWERS - 2:
+                    second_rows(face, both)
             else:
                 late_rows(face, both)
 
@@ -317,6 +319,15 @@
             zbuf[rows, :LANES] = hi.astype(bf16)
             zbuf[rows, LANES:] = lo.astype(bf16)
             newest[rows, :] = jnp.where(g64 < 2, hi, pltpu.roll(lo, LANES // 2, 1)).astype(bf16)
+
+    def second_rows(face, newer):
+        rows = slice(face * DOF, (face + 1) * DOF)
+        hi, lo = split(ordered[1, face] + newer)
+        hi, lo = hi.astype(bf16), lo.astype(bf16)
+        second = g64 == 1
+        zbuf[rows, :LANES] = jnp.where(second, hi, zbuf[rows, :LANES])
+        zbuf[rows, LANES:] = jnp.where(second, lo, zbuf[rows, LANES:])
+        newest[rows, :] = jnp.where(second, hi, jnp.where(g64 == 3, lo, newest[rows, :]))
 
     def late_rows(face, newer):
         rows = slice(face * DOF, (face + 1) * DOF)
@@ -410,16 +421,6 @@
         return jnp.concatenate([final[rank] for rank in range(plane)], axis=0)
 
     def early_gram():
-        @pl.loop(0, faces, unroll=4)
-        def _(face):
-            rows = pl.ds(pl.multiple_of(face * DOF, DOF), DOF)
-            hi, lo = split(ordered[1, face] + ordered[2, face])
-            hi, lo = hi.astype(bf16), lo.astype(bf16)
-            second = g64 == 1
-            zbuf[rows, :LANES] = jnp.where(second, hi, zbuf[rows, :LANES])
-            zbuf[rows, LANES:] = jnp.where(second, lo, zbuf[rows, LANES:])
-            newest[rows, :] = jnp.where(second, hi, jnp.where(g64 == 3, lo, newest[rows, :]))
-
         both = lax.dot_general(newest[...], zbuf[...], (((0,), (0,)), ((), ())), preferred_element_type=f32)
         half = 2 * NRHS
         gram = (both[:half, :LANES] + both[half:, LANES:]) + (both[:half, LANES:] + both[half:, :LANES])
@@ -487,10 +488,10 @@
                 send_field(power + 1, copies, (2, 3))
         else:
             with scope("far%d" % power):
-                far_products(power, range(faces // 2))
+                far_products(power, range(faces // 4))
                 with scope("eplane"):
                     exchange(0, early_line, scatter_sum(0, early_buf, early_plane))
-                far_products(power, range(faces // 2, faces))
+                far_products(power, range(faces // 4, faces))
 
     with scope("lgram"):
         late_gram()

time: 28.8 us -> 28.8 us (level)
  no operation moved by 1% of the time
where the time goes in v8:
time: 28.8 us; the launch traced here: 28.6 us
  Pallas kernels  28 us (97%)
  between operations  0.64 us (2%)
    pallas_call x1, Pallas kernels, on_device(): pl.pallas_call(functools.partial(kernel, shape), out_shape=(out, out), in...  27.2 us
    pallas_call x1, Pallas kernels, on_device(): pl.pallas_call(put_out, out_shape=(out, out), in_specs=[vmem, vmem], out_...  0.72 us

profile of v8, /device:TPU:0, one launch (start us, length us, event | category | flops | bytes accessed | tf_op | source)
XLA Modules:
  0.0 28.6 jit_solution(7126927205350918189)
XLA Ops:
  0.6 27.2 %shard_map.59 = (f32[16,2048]{1,0:T(8,128)S(1)}, f32[16,2048]{1,0:T(8,128)S(1)}) custom-call(f32[2,16,8,128]{3,2,1,0:T(8,128)} %bitcast.7, f32[11,2,32,8,128]{4,3,2,1,0:T(8,128)} %bitcast.6, s32[16,11]{1,0:T(8,128)} %columns_hbm.1, s32[4,4]{1,0:T(4,128)} %ghost_hbm.1), custom_call_target="tpu_custom_call" | custom-call | tf_op jit(solution)/shard_map/pallas_call | solution.py:593
  27.9 0.7 %shard_map.60 = (f32[16,2048]{1,0:T(8,128)}, f32[16,2048]{1,0:T(8,128)}) custom-call(f32[16,2048]{1,0:T(8,128)S(1)} %get-tuple-element.4.sol_ref, f32[16,2048]{1,0:T(8,128)S(1)} %get-tuple-element.5.res_ref), custom_call_target="tpu_custom_call" | custom-call | tf_op jit(solution)/shard_map/pallas_call | solution.py:629
